TPU v7x, 32 devices: a whole 2x2x4 slice. The times are simulated.
32 devices in a mesh: rep: 4 (over y, x), grp: 8 (over z, core).
Axes of the slice: x: 2, y: 2, z: 4, core: 2. Of those that a mesh axis runs over, the one named last changes fastest.
Arguments:
- tokens: bfloat16 [8, 4096, 384], P('rep', 'grp'), may hold values from -6 to 6
- segment_ids: int32 [8, 4096], P('rep', 'grp'), may hold values from 0 to 7, never falling along the last dimension, each value on 1 to 2048 neighbouring positions
- out_grad: bfloat16 [8, 4096, 384], P('rep', 'grp'), may hold values from -6 to 6
- query_weight: bfloat16 [384, 384], P('grp'), may hold values from -0.3125 to 0.3125
- key_weight: bfloat16 [384, 384], P('grp'), may hold values from -0.3125 to 0.3125
- value_weight: bfloat16 [384, 384], P('grp'), may hold values from -0.3125 to 0.3125
- output_weight: bfloat16 [384, 384], P('grp'), may hold values from -3.5 to 3.5
- inner_weight: bfloat16 [384, 1536], P('grp'), may hold values from -0.3125 to 0.3125
- outer_weight: bfloat16 [1536, 384], P('grp'), may hold values from -0.15625 to 0.15625
- query_bias: bfloat16 [384], P('grp'), may hold values from -3 to 3
- value_bias: bfloat16 [384], P('grp'), may hold values from -3 to 3
- output_bias: bfloat16 [384], P('grp'), may hold values from -3 to 3
- inner_bias: bfloat16 [1536], P('grp'), may hold values from -3 to 3
- outer_bias: bfloat16 [384], P('grp'), may hold values from -3 to 3
- first_gain: bfloat16 [384], P('grp'), may hold values from 0.25 to 1.75
- first_shift: bfloat16 [384], P('grp'), may hold values from -3 to 3
- second_gain: bfloat16 [384], P('grp'), may hold values from 0.25 to 1.75
- second_shift: bfloat16 [384], P('grp'), may hold values from -3 to 3
Outputs:
- layer_out: bfloat16 [8, 4096, 384], P('rep', 'grp')
- input_grad: bfloat16 [8, 4096, 384], P('rep', 'grp')
- grad_query_weight: float32 [384, 384], P('grp')
- grad_key_weight: float32 [384, 384], P('grp')
- grad_value_weight: float32 [384, 384], P('grp')
- grad_output_weight: float32 [384, 384], P('grp')
- grad_inner_weight: float32 [384, 1536], P('grp')
- grad_outer_weight: float32 [1536, 384], P('grp')
- grad_query_bias: float32 [384], P('grp')
- grad_value_bias: float32 [384], P('grp')
- grad_output_bias: float32 [384], P('grp')
- grad_inner_bias: float32 [1536], P('grp')
- grad_outer_bias: float32 [384], P('grp')
- grad_first_gain: float32 [384], P('grp')
- grad_first_shift: float32 [384], P('grp')
- grad_second_gain: float32 [384], P('grp')
- grad_second_shift: float32 [384], P('grp')
Inputs may be any that keep to these rules, and one draw needn't show every extreme that they name: `segment_ids`: along each sequence the ids never fall; each of the 8 ids marks one document of 1 to 2048 tokens, and one document of each sequence holds exactly 2048 tokens.
All inputs are finite; a program needn't handle non-finite values.
Results may differ from a plain program's by a relative error of at most 0.015.
Values may be sent and summed in bfloat16 or wider, within the bound.
A program may use at most 320 MiB of HBM per device.

v0:
```python
from functools import reduce

import jax
import jax.numpy as jnp
from jax import lax
from jax.sharding import PartitionSpec as P

H = 12
MICRO = 2
SEQ_MB = 1


norm_epsilon = 1e-05
masked_score = -1000000000.0


def layer_norm(inputs, norm_gain, norm_shift):
    center = inputs - jnp.mean(inputs, axis=-1, keepdims=True)
    spread = jnp.mean(center * center, axis=-1, keepdims=True)
    return center * lax.rsqrt(spread + norm_epsilon) * norm_gain + norm_shift


def exact_gelu(inputs):
    return jax.nn.gelu(inputs, approximate=False)


def times_transpose(left, right):
    return lax.dot_general(
        left, right, (((1,), (1,)), ((), ())), preferred_element_type=jnp.float32
    )


def transpose_times(left, right):
    return lax.dot_general(
        left, right, (((0,), (0,)), ((), ())), preferred_element_type=jnp.float32
    )


def column_total(inputs):
    return jnp.sum(inputs.astype(jnp.float32), axis=0)


def masked_scores(query_group, key_group, same_doc, score_scale):
    scores = (
        jnp.einsum("bqhd,bkhd->bhqk", query_group, key_group, preferred_element_type=jnp.float32)
        * score_scale
    )
    return jnp.where(same_doc[:, None], scores, masked_score)


def group_forward(query_group, key_group, value_group, same_doc, score_scale):
    scores = masked_scores(query_group, key_group, same_doc, score_scale)
    highest = jnp.max(scores, axis=-1, keepdims=True)
    log_total = highest + jnp.log(jnp.sum(jnp.exp(scores - highest), axis=-1, keepdims=True))
    weights_low = jnp.exp(scores - log_total).astype(jnp.bfloat16)
    context = jnp.einsum(
        "bhqk,bkhd->bqhd", weights_low, value_group, preferred_element_type=jnp.float32
    )
    return (context.astype(jnp.bfloat16), log_total)


def group_backward(
    query_group, key_group, value_group, same_doc, log_total, grad_context, score_scale
):
    attn_weights = jnp.exp(masked_scores(query_group, key_group, same_doc, score_scale) - log_total)
    weights_low = attn_weights.astype(jnp.bfloat16)
    grad_weights = jnp.einsum(
        "bqhd,bkhd->bhqk", grad_context, value_group, preferred_element_type=jnp.float32
    )
    centre = jnp.sum(attn_weights * grad_weights, axis=-1, keepdims=True)
    grad_scores = (attn_weights * (grad_weights - centre)).astype(jnp.bfloat16)
    grad_query = jnp.einsum(
        "bhqk,bkhd->bqhd", grad_scores, key_group, preferred_element_type=jnp.float32
    )
    grad_query = (grad_query * score_scale).astype(jnp.bfloat16)
    grad_key = (
        jnp.einsum("bhqk,bqhd->bkhd", grad_scores, query_group, preferred_element_type=jnp.float32)
        * score_scale
    )
    grad_value = jnp.einsum(
        "bhqk,bqhd->bkhd", weights_low, grad_context, preferred_element_type=jnp.float32
    )
    return (grad_query, grad_key, grad_value)


def merge_groups(stacked, row_total, model_width):
    return jnp.moveaxis(stacked, 0, 2).reshape(row_total, model_width)


def gradient_terms(
    token_rows,
    context_rows,
    hidden_rows,
    active_rows,
    grad_queries,
    grad_keys,
    grad_values,
    grad_attention,
    grad_inner,
    grad_feed,
    norm_grads,
):
    return (
        transpose_times(token_rows, grad_queries),
        transpose_times(token_rows, grad_keys),
        transpose_times(token_rows, grad_values),
        transpose_times(context_rows, grad_attention),
        transpose_times(hidden_rows, grad_inner),
        transpose_times(active_rows, grad_feed),
        column_total(grad_queries),
        column_total(grad_values),
        column_total(grad_attention),
        column_total(grad_inner),
        column_total(grad_feed),
        norm_grads[0],
        norm_grads[1],
        norm_grads[2],
        norm_grads[3],
    )


def on_device(
    tokens,
    segment_ids,
    out_grad,
    query_weight,
    key_weight,
    value_weight,
    output_weight,
    inner_weight,
    outer_weight,
    query_bias,
    value_bias,
    output_bias,
    inner_bias,
    outer_bias,
    first_gain,
    first_shift,
    second_gain,
    second_shift,
):
    row_count = tokens.shape[1]
    model_width = tokens.shape[2]
    head_count = H
    head_size = model_width // head_count
    per_group = max(1, min(head_count, 128 // head_size))
    group_width = per_group * head_size
    group_count = head_count // per_group
    score_scale = head_size ** (-0.5)
    seq_count = SEQ_MB
    flat_rows = seq_count * row_count
    all_segments = lax.all_gather(segment_ids, "grp", axis=1, tiled=True)
    outputs = []
    input_grads = []
    shares_list = []
    for batch_index in range(MICRO):
        offset = batch_index * seq_count
        local_tokens = tokens[offset : offset + seq_count]
        flat_tokens = local_tokens.reshape(flat_rows, model_width)
        gathered = (
            lax.all_gather(query_weight, "grp", axis=0, tiled=True),
            lax.all_gather(key_weight, "grp", axis=0, tiled=True),
            lax.all_gather(value_weight, "grp", axis=0, tiled=True),
            lax.all_gather(output_weight, "grp", axis=0, tiled=True),
            lax.all_gather(inner_weight, "grp", axis=0, tiled=True),
            lax.all_gather(outer_weight, "grp", axis=0, tiled=True),
            lax.all_gather(query_bias, "grp", axis=0, tiled=True),
            lax.all_gather(value_bias, "grp", axis=0, tiled=True),
            lax.all_gather(output_bias, "grp", axis=0, tiled=True),
            lax.all_gather(inner_bias, "grp", axis=0, tiled=True),
            lax.all_gather(outer_bias, "grp", axis=0, tiled=True),
            lax.all_gather(first_gain, "grp", axis=0, tiled=True),
            lax.all_gather(first_shift, "grp", axis=0, tiled=True),
            lax.all_gather(second_gain, "grp", axis=0, tiled=True),
            lax.all_gather(second_shift, "grp", axis=0, tiled=True),
        )
        full_query, full_key, full_value, full_output, full_inner, full_outer = gathered[:6]
        (
            bias_query,
            bias_value,
            bias_output,
            bias_inner,
            bias_outer,
            gain_first,
            shift_first,
            gain_second,
            shift_second,
        ) = [vector.astype(jnp.float32) for vector in gathered[6:]]
        queries = (
            jnp.dot(flat_tokens, full_query, preferred_element_type=jnp.float32) + bias_query
        ).astype(jnp.bfloat16)
        key_rows = jnp.dot(flat_tokens, full_key, preferred_element_type=jnp.float32).astype(
            jnp.bfloat16
        )
        value_rows = (
            jnp.dot(flat_tokens, full_value, preferred_element_type=jnp.float32) + bias_value
        ).astype(jnp.bfloat16)
        key_split = key_rows.reshape(seq_count, row_count, model_width)
        value_split = value_rows.reshape(seq_count, row_count, model_width)
        key_all, value_all = (
            lax.all_gather(key_split, "grp", axis=1, tiled=True),
            lax.all_gather(value_split, "grp", axis=1, tiled=True),
        )
        length = key_all.shape[1]
        local_segments = segment_ids[offset : offset + seq_count]
        far_segments = all_segments[offset : offset + seq_count]
        same_doc = local_segments[:, :, None] == far_segments[:, None, :]
        query_split = queries.reshape(seq_count, row_count, model_width)

        def slice_group(array, group_index):
            piece = lax.dynamic_slice_in_dim(array, group_index * group_width, group_width, 2)
            return piece.reshape(array.shape[0], array.shape[1], per_group, head_size)

        def forward_group(group_index):
            context, log_total = group_forward(
                slice_group(query_split, group_index),
                slice_group(key_all, group_index),
                slice_group(value_all, group_index),
                same_doc,
                score_scale,
            )
            return (context.reshape(seq_count, row_count, group_width), log_total)

        context_groups, log_totals = lax.map(forward_group, jnp.arange(group_count))
        context_rows = merge_groups(context_groups, flat_rows, model_width)
        attention = (
            jnp.dot(context_rows, full_output, preferred_element_type=jnp.float32) + bias_output
        )
        residual_one = flat_tokens.astype(jnp.float32) + attention
        hidden_one, norm_one_pullback = jax.vjp(layer_norm, residual_one, gain_first, shift_first)
        hidden_low = hidden_one.astype(jnp.bfloat16)
        inner_pre = jnp.dot(hidden_low, full_inner, preferred_element_type=jnp.float32) + bias_inner
        activation, gelu_pullback = jax.vjp(exact_gelu, inner_pre)
        active_low = activation.astype(jnp.bfloat16)
        feed = jnp.dot(active_low, full_outer, preferred_element_type=jnp.float32) + bias_outer
        output_rows, norm_two_pullback = jax.vjp(
            layer_norm, hidden_one + feed, gain_second, shift_second
        )
        outputs.append(output_rows.astype(jnp.bfloat16).reshape(seq_count, row_count, model_width))
        cotangent = (
            out_grad[offset : offset + seq_count]
            .reshape(flat_rows, model_width)
            .astype(jnp.float32)
        )
        grad_two, grad_gain_two, grad_shift_two = norm_two_pullback(cotangent)
        grad_feed = grad_two.astype(jnp.bfloat16)
        grad_active = times_transpose(grad_feed, full_outer)
        grad_inner = gelu_pullback(grad_active)[0].astype(jnp.bfloat16)
        grad_hidden = grad_two + times_transpose(grad_inner, full_inner)
        grad_one, grad_gain_one, grad_shift_one = norm_one_pullback(grad_hidden)
        grad_attention = grad_one.astype(jnp.bfloat16)
        grad_context = times_transpose(grad_attention, full_output).astype(jnp.bfloat16)
        grad_context = grad_context.reshape(seq_count, row_count, model_width)

        def backward_group(pieces):
            group_index, log_total = pieces
            grad_query, grad_key, grad_value = group_backward(
                slice_group(query_split, group_index),
                slice_group(key_all, group_index),
                slice_group(value_all, group_index),
                same_doc,
                log_total,
                slice_group(grad_context, group_index),
                score_scale,
            )
            return (
                grad_query.reshape(seq_count, row_count, group_width),
                grad_key.reshape(seq_count, length, group_width),
                grad_value.reshape(seq_count, length, group_width),
            )

        query_groups, key_groups, value_groups = lax.map(
            backward_group, (jnp.arange(group_count), log_totals)
        )
        key_owned, value_owned = (
            lax.psum_scatter(key_groups, "grp", scatter_dimension=2, tiled=True),
            lax.psum_scatter(value_groups, "grp", scatter_dimension=2, tiled=True),
        )
        grad_keys = merge_groups(key_owned, flat_rows, model_width).astype(jnp.bfloat16)
        grad_values = merge_groups(value_owned, flat_rows, model_width).astype(jnp.bfloat16)
        grad_queries = merge_groups(query_groups, flat_rows, model_width)
        grad_tokens = (
            grad_one
            + times_transpose(grad_queries, full_query)
            + times_transpose(grad_keys, full_key)
            + times_transpose(grad_values, full_value)
        )
        input_grads.append(
            grad_tokens.astype(jnp.bfloat16).reshape(seq_count, row_count, model_width)
        )
        norm_grads = (grad_gain_one, grad_shift_one, grad_gain_two, grad_shift_two)
        terms = gradient_terms(
            flat_tokens,
            context_rows,
            hidden_low,
            active_low,
            grad_queries,
            grad_keys,
            grad_values,
            grad_attention,
            grad_inner,
            grad_feed,
            norm_grads,
        )
        shares = (
            lax.psum_scatter(terms[0], "grp", scatter_dimension=0, tiled=True),
            lax.psum_scatter(terms[1], "grp", scatter_dimension=0, tiled=True),
            lax.psum_scatter(terms[2], "grp", scatter_dimension=0, tiled=True),
            lax.psum_scatter(terms[3], "grp", scatter_dimension=0, tiled=True),
            lax.psum_scatter(terms[4], "grp", scatter_dimension=0, tiled=True),
            lax.psum_scatter(terms[5], "grp", scatter_dimension=0, tiled=True),
            lax.psum_scatter(terms[6], "grp", scatter_dimension=0, tiled=True),
            lax.psum_scatter(terms[7], "grp", scatter_dimension=0, tiled=True),
            lax.psum_scatter(terms[8], "grp", scatter_dimension=0, tiled=True),
            lax.psum_scatter(terms[9], "grp", scatter_dimension=0, tiled=True),
            lax.psum_scatter(terms[10], "grp", scatter_dimension=0, tiled=True),
            lax.psum_scatter(terms[11], "grp", scatter_dimension=0, tiled=True),
            lax.psum_scatter(terms[12], "grp", scatter_dimension=0, tiled=True),
            lax.psum_scatter(terms[13], "grp", scatter_dimension=0, tiled=True),
            lax.psum_scatter(terms[14], "grp", scatter_dimension=0, tiled=True),
        )
        shares_list.append(shares)
    owned = reduce(
        lambda left_part, right_part: jax.tree.map(jnp.add, left_part, right_part), shares_list
    )
    summed = (
        lax.psum(owned[0].astype(jnp.bfloat16), "rep").astype(jnp.float32),
        lax.psum(owned[1].astype(jnp.bfloat16), "rep").astype(jnp.float32),
        lax.psum(owned[2].astype(jnp.bfloat16), "rep").astype(jnp.float32),
        lax.psum(owned[3].astype(jnp.bfloat16), "rep").astype(jnp.float32),
        lax.psum(owned[4].astype(jnp.bfloat16), "rep").astype(jnp.float32),
        lax.psum(owned[5].astype(jnp.bfloat16), "rep").astype(jnp.float32),
        lax.psum(owned[6].astype(jnp.bfloat16), "rep").astype(jnp.float32),
        lax.psum(owned[7].astype(jnp.bfloat16), "rep").astype(jnp.float32),
        lax.psum(owned[8].astype(jnp.bfloat16), "rep").astype(jnp.float32),
        lax.psum(owned[9].astype(jnp.bfloat16), "rep").astype(jnp.float32),
        lax.psum(owned[10].astype(jnp.bfloat16), "rep").astype(jnp.float32),
        lax.psum(owned[11].astype(jnp.bfloat16), "rep").astype(jnp.float32),
        lax.psum(owned[12].astype(jnp.bfloat16), "rep").astype(jnp.float32),
        lax.psum(owned[13].astype(jnp.bfloat16), "rep").astype(jnp.float32),
        lax.psum(owned[14].astype(jnp.bfloat16), "rep").astype(jnp.float32),
    )
    return (
        jnp.concatenate(outputs, axis=0),
        jnp.concatenate(input_grads, axis=0),
        summed[0],
        summed[1],
        summed[2],
        summed[3],
        summed[4],
        summed[5],
        summed[6],
        summed[7],
        summed[8],
        summed[9],
        summed[10],
        summed[11],
        summed[12],
        summed[13],
        summed[14],
    )


def solution(mesh):
    in_specs = (
        P("rep", "grp", None),
        P("rep", "grp"),
        P("rep", "grp", None),
        P("grp", None),
        P("grp", None),
        P("grp", None),
        P("grp", None),
        P("grp", None),
        P("grp", None),
        P("grp"),
        P("grp"),
        P("grp"),
        P("grp"),
        P("grp"),
        P("grp"),
        P("grp"),
        P("grp"),
        P("grp"),
    )
    out_specs = (
        P("rep", "grp", None),
        P("rep", "grp", None),
        P("grp", None),
        P("grp", None),
        P("grp", None),
        P("grp", None),
        P("grp", None),
        P("grp", None),
        P("grp"),
        P("grp"),
        P("grp"),
        P("grp"),
        P("grp"),
        P("grp"),
        P("grp"),
        P("grp"),
        P("grp"),
    )
    return jax.shard_map(
        on_device, mesh=mesh, in_specs=in_specs, out_specs=out_specs, check_vma=False
    )
```

profile of v0, /device:TPU:0, one launch (start us, length us, event | category | flops | bytes accessed | tf_op | source)
XLA Modules:
  0.0 1719.2 jit_solution(15107019343123948251)
XLA Ops:
  17.5 30.2 %all-reduce.19 = (bf16[384]{0:T(512)(128)(2,1)S(1)}, bf16[384]{0:T(512)(128)(2,1)S(1)}, bf16[1536]{0:T(1024)(128)(2,1)S(1)}, bf16[384]{0:T(512)(128)(2,1)S(1)}, ...) all-reduce(bf16[384]{0:T(512)(128)(2,1)S(1)} %dynamic-update-slice., ...), channel_id=1, replica_groups=mesh['rep'=4,'grp'=8] {'grp'}, use_global_device_ids=true, to_apply=%add.1 | all-reduce | flops 4608 | bytes 18432
  47.8 14.4 all_gather.75
  64.6 15.2 all_gather.81
  85.8 14.3 all_gather.78
  100.8 14.3 all_gather.79
  118.4 16.6 all_gather.83
  154.0 156.3 %while.56 = (s32[]{:T(128)}, bf16[3,1,512,128]{2,3,1,0:T(8,128)(2,1)S(1)}, f32[3,1,4,512,1]{3,2,4,1,0:T(4,128)}, s32[3]{0:T(128)}, bf16[1,4096,384]{1,2,0:T(8,12...) while((s32[]{:T(128)}, ...), condition=%wide.region_3.4_spmd.clone, body=%wide.region_0.3_spmd.clone.sunk | while | flops 1168177152 | bytes 116222688 | solution.py:224
  159.9 14.5 fusion.255
  174.3 15.1 exponential_reduce_fusion.4
  190.1 15.1 fusion.256
  212.0 14.4 fusion.255
  226.4 15.5 exponential_reduce_fusion.4
  242.5 15.2 fusion.256
  264.5 14.2 fusion.255
  278.8 15.1 exponential_reduce_fusion.4
  294.5 15.0 fusion.256
  337.2 153.2 %while.57 = (s32[]{:T(128)}, bf16[3,1,512,128]{2,3,1,0:T(8,128)(2,1)}, f32[3,1,4,512,1]{3,2,4,1,0:T(4,128)S(1)}, s32[3]{0:T(128)S(1)}, bf16[1,4096,384]{1,2,0:T(...) while((s32[]{:T(128)}, ...), condition=%wide.region_11.12_spmd.clone, body=%wide.region_8.11_spmd.clone.sunk | while | flops 1168177152 | bytes 116214464 | solution.py:224
  342.3 14.2 fusion.260
  356.6 15.1 exponential_reduce_fusion.5
  371.7 15.0 fusion.261
  393.4 14.2 fusion.260
  407.6 15.1 exponential_reduce_fusion.5
  422.7 15.0 fusion.261
  444.4 14.2 fusion.260
  458.7 15.1 exponential_reduce_fusion.5
  473.8 15.0 fusion.261
  492.1 11.0 multiply_convert_fusion.2
  541.3 348.5 %while.58 = (s32[]{:T(128)}, bf16[3,1,512,128]{2,3,1,0:T(8,128)(2,1)}, f32[3,1,4096,128]{2,3,1,0:T(8,128)}, f32[3,1,4096,128]{2,3,1,0:T(8,128)}, s32[3]{0:T(128)...) while((s32[]{:T(128)}, ...), condition=%wide.region_22.23_spmd.clone, body=%wide.region_20.22_spmd.clone.sunk | while | flops 2812934144 | bytes 281750752 | solution.py:272
  545.1 13.4 fusion.272
  562.9 24.8 %multiply_reduce_fusion.12 = (f32[4,512]{1,0:T(4,128)S(1)}, f32[4,512,4096]{2,1,0:T(8,128)}) fusion(f32[4,512,4096]{2,1,0:T(8,128)} %fusion.272, f32[4,512]{1,0:T(4,128)S(1)} %dynamic-slice_bitcast_fusion.4, pred[512,4096]{1,0:T(8,128)(4,1)S(1)} %compare_bitcast_fusion.10, bf16[512,4,32]{0,2,1:T(8,128)(2,1)S(1)} %bitcast.444, ...), kind=kOutput, calls=%fused_computation.37.clone.1 | convolution fusion | flops 578811904 | bytes 70402048 | tf_op jit(solution)/shard_map/while/body/eval_jaxpr/bqhd,bkhd->bhqk/dot_general | solution.py:67
  587.7 27.7 %multiply_convert_fusion.6 = bf16[4,512,4096]{2,1,0:T(8,128)(2,1)} fusion(f32[4,512,4096]{2,1,0:T(8,128)} %get-tuple-element.940, f32[4,512,4096]{2,1,0:T(8,128)} %fusion.272, f32[4,512]{1,0:T(4,128)S(1)} %get-tuple-element.941, f32[4,512]{1,0:T(4,128)S(1)} %dynamic-slice_bitcast_fusion.4, pred[512,4096]{1,0:T(8,128)(4,1)S(1)} %compare_bitcast_fusion.10), kind=kLoop, calls=%fused_computation.36.clone.1 | loop fusion | flops 50331648 | bytes 85999616 | tf_op jit(solution)/shard_map/while/body/eval_jaxpr/convert_element_type | solution.py:71
  625.4 16.3 fusion.274
  661.5 13.2 fusion.272
  679.0 24.7 %multiply_reduce_fusion.12 = (f32[4,512]{1,0:T(4,128)S(1)}, f32[4,512,4096]{2,1,0:T(8,128)}) fusion(f32[4,512,4096]{2,1,0:T(8,128)} %fusion.272, f32[4,512]{1,0:T(4,128)S(1)} %dynamic-slice_bitcast_fusion.4, pred[512,4096]{1,0:T(8,128)(4,1)S(1)} %compare_bitcast_fusion.10, bf16[512,4,32]{0,2,1:T(8,128)(2,1)S(1)} %bitcast.444, ...), kind=kOutput, calls=%fused_computation.37.clone.1 | convolution fusion | flops 578811904 | bytes 70402048 | tf_op jit(solution)/shard_map/while/body/eval_jaxpr/bqhd,bkhd->bhqk/dot_general | solution.py:67
  703.7 27.7 %multiply_convert_fusion.6 = bf16[4,512,4096]{2,1,0:T(8,128)(2,1)} fusion(f32[4,512,4096]{2,1,0:T(8,128)} %get-tuple-element.940, f32[4,512,4096]{2,1,0:T(8,128)} %fusion.272, f32[4,512]{1,0:T(4,128)S(1)} %get-tuple-element.941, f32[4,512]{1,0:T(4,128)S(1)} %dynamic-slice_bitcast_fusion.4, pred[512,4096]{1,0:T(8,128)(4,1)S(1)} %compare_bitcast_fusion.10), kind=kLoop, calls=%fused_computation.36.clone.1 | loop fusion | flops 50331648 | bytes 85999616 | tf_op jit(solution)/shard_map/while/body/eval_jaxpr/convert_element_type | solution.py:71
  741.4 16.3 fusion.274
  777.4 13.2 fusion.272
  794.9 24.7 %multiply_reduce_fusion.12 = (f32[4,512]{1,0:T(4,128)S(1)}, f32[4,512,4096]{2,1,0:T(8,128)}) fusion(f32[4,512,4096]{2,1,0:T(8,128)} %fusion.272, f32[4,512]{1,0:T(4,128)S(1)} %dynamic-slice_bitcast_fusion.4, pred[512,4096]{1,0:T(8,128)(4,1)S(1)} %compare_bitcast_fusion.10, bf16[512,4,32]{0,2,1:T(8,128)(2,1)S(1)} %bitcast.444, ...), kind=kOutput, calls=%fused_computation.37.clone.1 | convolution fusion | flops 578811904 | bytes 70402048 | tf_op jit(solution)/shard_map/while/body/eval_jaxpr/bqhd,bkhd->bhqk/dot_general | solution.py:67
  819.6 27.7 %multiply_convert_fusion.6 = bf16[4,512,4096]{2,1,0:T(8,128)(2,1)} fusion(f32[4,512,4096]{2,1,0:T(8,128)} %get-tuple-element.940, f32[4,512,4096]{2,1,0:T(8,128)} %fusion.272, f32[4,512]{1,0:T(4,128)S(1)} %get-tuple-element.941, f32[4,512]{1,0:T(4,128)S(1)} %dynamic-slice_bitcast_fusion.4, pred[512,4096]{1,0:T(8,128)(4,1)S(1)} %compare_bitcast_fusion.10), kind=kLoop, calls=%fused_computation.36.clone.1 | loop fusion | flops 50331648 | bytes 85999616 | tf_op jit(solution)/shard_map/while/body/eval_jaxpr/convert_element_type | solution.py:71
  857.3 16.3 fusion.274
  901.7 358.7 %while.59 = (s32[]{:T(128)}, bf16[3,1,512,128]{2,3,1,0:T(8,128)(2,1)}, f32[3,1,4096,128]{2,3,1,0:T(8,128)}, f32[3,1,4096,128]{2,3,1,0:T(8,128)}, s32[3]{0:T(128)...) while((s32[]{:T(128)}, ...), condition=%wide.region_31.32_spmd.clone, body=%wide.region_29.31_spmd.clone.sunk | while | flops 2812934144 | bytes 284896544 | solution.py:272
  917.8 13.4 fusion.285
  934.8 24.8 %multiply_reduce_fusion.13 = (f32[4,512]{1,0:T(4,128)S(1)}, f32[4,512,4096]{2,1,0:T(8,128)}) fusion(f32[4,512,4096]{2,1,0:T(8,128)} %fusion.285, f32[4,512]{1,0:T(4,128)S(1)} %dynamic-slice_bitcast_fusion.5, pred[512,4096]{1,0:T(8,128)(4,1)S(1)} %compare_bitcast_fusion.11, bf16[512,4,32]{0,2,1:T(8,128)(2,1)S(1)} %bitcast.446, ...), kind=kOutput, calls=%fused_computation.57.clone.1 | convolution fusion | flops 578811904 | bytes 70402048 | tf_op jit(solution)/shard_map/while/body/eval_jaxpr/bqhd,bkhd->bhqk/dot_general | solution.py:67
  959.6 27.8 %multiply_convert_fusion.7 = bf16[4,512,4096]{2,1,0:T(8,128)(2,1)} fusion(f32[4,512,4096]{2,1,0:T(8,128)} %get-tuple-element.956, f32[4,512,4096]{2,1,0:T(8,128)} %fusion.285, f32[4,512]{1,0:T(4,128)S(1)} %get-tuple-element.957, f32[4,512]{1,0:T(4,128)S(1)} %dynamic-slice_bitcast_fusion.5, pred[512,4096]{1,0:T(8,128)(4,1)S(1)} %compare_bitcast_fusion.11), kind=kLoop, calls=%fused_computation.56.clone.1 | loop fusion | flops 50331648 | bytes 85999616 | tf_op jit(solution)/shard_map/while/body/eval_jaxpr/convert_element_type | solution.py:71
  997.4 16.3 fusion.287
  1018.3 10.9 fusion.286
  1033.5 13.2 fusion.285
  1050.1 24.7 %multiply_reduce_fusion.13 = (f32[4,512]{1,0:T(4,128)S(1)}, f32[4,512,4096]{2,1,0:T(8,128)}) fusion(f32[4,512,4096]{2,1,0:T(8,128)} %fusion.285, f32[4,512]{1,0:T(4,128)S(1)} %dynamic-slice_bitcast_fusion.5, pred[512,4096]{1,0:T(8,128)(4,1)S(1)} %compare_bitcast_fusion.11, bf16[512,4,32]{0,2,1:T(8,128)(2,1)S(1)} %bitcast.446, ...), kind=kOutput, calls=%fused_computation.57.clone.1 | convolution fusion | flops 578811904 | bytes 70402048 | tf_op jit(solution)/shard_map/while/body/eval_jaxpr/bqhd,bkhd->bhqk/dot_general | solution.py:67
  1074.8 27.7 %multiply_convert_fusion.7 = bf16[4,512,4096]{2,1,0:T(8,128)(2,1)} fusion(f32[4,512,4096]{2,1,0:T(8,128)} %get-tuple-element.956, f32[4,512,4096]{2,1,0:T(8,128)} %fusion.285, f32[4,512]{1,0:T(4,128)S(1)} %get-tuple-element.957, f32[4,512]{1,0:T(4,128)S(1)} %dynamic-slice_bitcast_fusion.5, pred[512,4096]{1,0:T(8,128)(4,1)S(1)} %compare_bitcast_fusion.11), kind=kLoop, calls=%fused_computation.56.clone.1 | loop fusion | flops 50331648 | bytes 85999616 | tf_op jit(solution)/shard_map/while/body/eval_jaxpr/convert_element_type | solution.py:71
  1112.5 16.3 fusion.287
  1133.4 10.9 fusion.286
  1148.6 13.2 fusion.285
  1165.2 24.7 %multiply_reduce_fusion.13 = (f32[4,512]{1,0:T(4,128)S(1)}, f32[4,512,4096]{2,1,0:T(8,128)}) fusion(f32[4,512,4096]{2,1,0:T(8,128)} %fusion.285, f32[4,512]{1,0:T(4,128)S(1)} %dynamic-slice_bitcast_fusion.5, pred[512,4096]{1,0:T(8,128)(4,1)S(1)} %compare_bitcast_fusion.11, bf16[512,4,32]{0,2,1:T(8,128)(2,1)S(1)} %bitcast.446, ...), kind=kOutput, calls=%fused_computation.57.clone.1 | convolution fusion | flops 578811904 | bytes 70402048 | tf_op jit(solution)/shard_map/while/body/eval_jaxpr/bqhd,bkhd->bhqk/dot_general | solution.py:67
  1189.9 27.7 %multiply_convert_fusion.7 = bf16[4,512,4096]{2,1,0:T(8,128)(2,1)} fusion(f32[4,512,4096]{2,1,0:T(8,128)} %get-tuple-element.956, f32[4,512,4096]{2,1,0:T(8,128)} %fusion.285, f32[4,512]{1,0:T(4,128)S(1)} %get-tuple-element.957, f32[4,512]{1,0:T(4,128)S(1)} %dynamic-slice_bitcast_fusion.5, pred[512,4096]{1,0:T(8,128)(4,1)S(1)} %compare_bitcast_fusion.11), kind=kLoop, calls=%fused_computation.56.clone.1 | loop fusion | flops 50331648 | bytes 85999616 | tf_op jit(solution)/shard_map/while/body/eval_jaxpr/convert_element_type | solution.py:71
  1227.6 16.3 fusion.287
  1280.6 48.1 %reduce-scatter.23.cloned.1.call-done = f32[3,1,512,128]{2,3,1,0:T(8,128)} async-done(((f32[3,1,4096,128]{2,3,1,0:T(8,128)}), f32[3,1,512,128]{2,3,1,0:T(8,128)}) %reduce-scatter.23.cloned.1.call-update) | async-done | bytes 786448 | tf_op jit(solution)/shard_map/reduce_scatter | solution.py:277
  1340.1 59.0 %reduce-scatter.17.cloned.1.call-done = f32[3,1,512,128]{2,3,1,0:T(8,128)} async-done(((f32[3,1,4096,128]{2,3,1,0:T(8,128)}), f32[3,1,512,128]{2,3,1,0:T(8,128)}) %reduce-scatter.17.cloned.1.call-update) | async-done | bytes 786448 | tf_op jit(solution)/shard_map/reduce_scatter | solution.py:276
  1400.3 69.2 %reduce-scatter.21.cloned.1.call-done = f32[3,1,512,128]{2,3,1,0:T(8,128)} async-done(((f32[3,1,4096,128]{2,3,1,0:T(8,128)}), f32[3,1,512,128]{2,3,1,0:T(8,128)}) %reduce-scatter.21.cloned.1.call-update) | async-done | bytes 786448 | tf_op jit(solution)/shard_map/reduce_scatter | solution.py:276
  1474.6 26.6 %reduce-scatter.25.cloned.1.call-done = f32[48,384]{1,0:T(8,128)} async-done(((f32[384,384]{1,0:T(8,128)}), f32[48,384]{1,0:T(8,128)}) %reduce-scatter.25.cloned.1.call-update) | async-done | bytes 73744 | tf_op jit(solution)/shard_map/reduce_scatter | solution.py:309
  1502.7 30.1 %reduce-scatter.31.cloned.1.call-done = f32[48,384]{1,0:T(8,128)} async-done(((f32[384,384]{1,0:T(8,128)}), f32[48,384]{1,0:T(8,128)}) %reduce-scatter.31.cloned.1.call-update) | async-done | bytes 73744
  1534.4 43.5 %all-reduce.27.cloned.1.call-done = (bf16[48,1536]{1,0:T(8,128)(2,1)}, bf16[192,384]{1,0:T(8,128)(2,1)}) async-done(((bf16[48,1536]{1,0:T(8,128)(2,1)}, bf16[192,384]{1,0:T(8,128)(2,1)}), (bf16[48,1536]{1,0:T(8,128)(2,1)}, bf16[192,384]{1,0:T(8,128)(2,1)})) %all-reduce.27.cloned.1.call-update) | async-done | bytes 294928 | tf_op jit(solution)/shard_map/psum | solution.py:331
  1581.3 28.2 %all-reduce.18 = (bf16[384]{0:T(512)(128)(2,1)S(1)}, bf16[384]{0:T(512)(128)(2,1)S(1)}, bf16[384]{0:T(512)(128)(2,1)S(1)}, bf16[1536]{0:T(1024)(128)(2,1)S(1)}, ...) all-reduce(f32[384]{0:T(512)S(1)} %add_bitcast_fusion.1, ...), channel_id=31, replica_groups=mesh['rep'=4,'grp'=8] {'grp'}, use_global_device_ids=true, to_apply=%region_53.54.clone | all-reduce | flops 4608 | bytes 27648
  1618.7 24.2 %reduce-scatter.33.cloned.1.call-done = f32[48,384]{1,0:T(8,128)} async-done(((f32[384,384]{1,0:T(8,128)}), f32[48,384]{1,0:T(8,128)}) %reduce-scatter.33.cloned.1.call-update) | async-done | bytes 73744
  1646.2 49.5 %all-reduce.25.cloned.1.call-done = (bf16[48,384]{0,1:T(8,128)(2,1)}, bf16[48,384]{0,1:T(8,128)(2,1)}, bf16[48,384]{0,1:T(8,128)(2,1)}, bf16[48,384]{1,0:T(8,128...) async-done(((bf16[48,384]{0,1:T(8,128)(2,1)}, ...) | async-done | bytes 148624 | tf_op jit(solution)/shard_map/psum | solution.py:327
  (538 shorter events, 404.6 us)
Async XLA Ops:
  7.2 74.9 %copy-start = (bf16[2,512,384]{2,1,0:T(8,128)(2,1)S(1)}, bf16[2,512,384]{2,1,0:T(8,128)(2,1)}, u32[]{:S(2)}) copy-start(bf16[2,512,384]{2,1,0:T(8,128)(2,1)} %param.26) | copy-start | bytes 2359300
  7.2 136.1 %all-gather.15.cloned.1.call-start = ((), (), s32[]{:S(2)}) async-start(), calls=%async_computation.16 | async-start | bytes 3538944 | tf_op jit(solution)/shard_map/all_gather | solution.py:202
  62.2 23.4 %copy-start.32 = (bf16[384,384]{1,0:T(8,128)(2,1)}, bf16[384,384]{1,0:T(8,128)(2,1)S(1)}, u32[]{:S(2)}) copy-start(bf16[384,384]{1,0:T(8,128)(2,1)S(1)} %all_gather.75) | copy-start | bytes 884740
  62.2 23.5 %copy-start.70 = (s32[2,512]{1,0:T(2,128)S(1)}, s32[2,512]{1,0:T(2,128)}, u32[]{:S(2)}) copy-start(s32[2,512]{1,0:T(2,128)} %param.27) | copy-start | bytes 12292
  64.5 83.6 %all-gather.17.cloned.1.call-start = ((), (), s32[]{:S(2)}) async-start(), calls=%async_computation.17 | async-start | bytes 3538944 | tf_op jit(solution)/shard_map/all_gather | solution.py:201
  79.8 21.0 %copy-start.8 = (bf16[384,384]{1,0:T(8,128)(2,1)}, bf16[384,384]{1,0:T(8,128)(2,1)S(1)}, u32[]{:S(2)}) copy-start(bf16[384,384]{1,0:T(8,128)(2,1)S(1)} %all_gather.81) | copy-start | bytes 884740
  79.8 21.0 %copy-start.57 = (bf16[48,384]{1,0:T(8,128)(2,1)S(1)}, bf16[48,384]{1,0:T(8,128)(2,1)}, u32[]{:S(2)}) copy-start(bf16[48,384]{1,0:T(8,128)(2,1)} %param.29) | copy-start | bytes 110596
  82.1 228.3 %all-gather.19.cloned.1.call-start = ((), (), s32[]{:S(2)}) async-start(), calls=%async_computation.18 | async-start | bytes 3538944 | tf_op jit(solution)/shard_map/all_gather | solution.py:202
  83.3 233.4 %all-gather.11.cloned.1.call-start = ((), (), s32[]{:S(2)}) async-start(), calls=%async_computation.10 | async-start | bytes 1327104 | tf_op jit(solution)/shard_map/all_gather | solution.py:165
  83.9 243.5 %all-gather.13.cloned.1.call-start = ((), (), s32[]{:S(2)}) async-start(), calls=%async_computation.11 | async-start | bytes 1327104 | tf_op jit(solution)/shard_map/all_gather | solution.py:166
  84.4 33.9 %copy-start.58 = (bf16[48,384]{1,0:T(8,128)(2,1)S(1)}, bf16[48,384]{1,0:T(8,128)(2,1)}, u32[]{:S(2)}) copy-start(bf16[48,384]{1,0:T(8,128)(2,1)} %param.32) | copy-start | bytes 110596
  84.5 247.1 %all-gather.21.cloned.1.call-start = ((), (), s32[]{:S(2)}) async-start(), calls=%async_computation.19 | async-start | bytes 3538944 | tf_op jit(solution)/shard_map/all_gather | solution.py:201
  85.7 53.2 %copy-start.44 = (bf16[2,512,384]{2,1,0:T(8,128)(2,1)S(1)}, bf16[2,512,384]{2,1,0:T(8,128)(2,1)}, u32[]{:S(2)}) copy-start(bf16[2,512,384]{2,1,0:T(8,128)(2,1)} %param.28) | copy-start | bytes 2359300
  85.7 1188.4 %reduce-scatter.29.cloned.1.call-start = ((), (), s32[]{:S(2)}) async-start(), calls=%async_computation.22 | async-start | bytes 2654208 | tf_op jit(solution)/shard_map/reduce_scatter | solution.py:311
  315.8 11.6 copy-start.2
  315.8 11.6 copy-start.55
  316.7 10.7 copy-start.60
  316.7 10.7 copy-start.97
  327.4 8.9 copy-start.18
  337.1 153.2 %copy-start.11 = (bf16[384,384]{1,0:T(8,128)(2,1)S(1)}, bf16[384,384]{1,0:T(8,128)(2,1)}, u32[]{:S(2)}) copy-start(bf16[384,384]{1,0:T(8,128)(2,1)} %all_gather.83) | copy-start | bytes 884740
  337.1 153.2 %copy-start.67 = (f32[384]{0:T(512)S(1)}, f32[384]{0:T(512)}, u32[]{:S(2)}) copy-start(f32[384]{0:T(512)} %convert_element_type.356) | copy-start | bytes 4612
  337.1 154.9 %copy-start.51 = (f32[384]{0:T(512)S(1)}, f32[384]{0:T(512)}, u32[]{:S(2)}) copy-start(f32[384]{0:T(512)} %convert_element_type.357) | copy-start | bytes 4612
  337.1 154.9 %copy-start.53 = (f32[384]{0:T(512)S(1)}, f32[384]{0:T(512)}, u32[]{:S(2)}) copy-start(f32[384]{0:T(512)} %convert_element_type.358) | copy-start | bytes 4612
  337.1 154.9 %copy-start.91 = (f32[1536]{0:T(1024)S(1)}, f32[1536]{0:T(1024)}, u32[]{:S(2)}) copy-start(f32[1536]{0:T(1024)} %convert_element_type.360) | copy-start | bytes 18436
  490.3 12.8 copy-start.49
  492.1 11.0 copy-start.98
  492.1 11.0 copy-start.100
  512.6 763.2 %reduce-scatter.27.cloned.1.call-start = ((), (), s32[]{:S(2)}) async-start(), calls=%async_computation.21 | async-start | bytes 2654208 | tf_op jit(solution)/shard_map/reduce_scatter | solution.py:310
  533.6 743.9 %reduce-scatter.19.cloned.1.call-start = ((), (), s32[]{:S(2)}) async-start(), calls=%async_computation.13 | async-start | bytes 7077888 | tf_op jit(solution)/shard_map/reduce_scatter | solution.py:277
  541.3 348.5 %copy-start.81 = (f32[512]{0:T(512)S(1)}, f32[512]{0:T(512)}, u32[]{:S(2)}) copy-start(f32[512]{0:T(512)} %get-tuple-element.635) | copy-start | bytes 6148
  893.9 434.7 %reduce-scatter.23.cloned.1.call-start = ((), (), s32[]{:S(2)}) async-start(), calls=%async_computation.15 | async-start | bytes 7077888 | tf_op jit(solution)/shard_map/reduce_scatter | solution.py:277
  914.3 17.0 copy-start.29
  1018.3 11.6 copy-start.30
  1029.9 16.7 copy-start.29
  1133.4 11.6 copy-start.30
  1145.0 16.7 copy-start.29
  1248.6 11.6 copy-start.30
  1260.4 138.7 %reduce-scatter.17.cloned.1.call-start = ((), (), s32[]{:S(2)}) async-start(), calls=%async_computation.12 | async-start | bytes 7077888 | tf_op jit(solution)/shard_map/reduce_scatter | solution.py:276
  1261.1 208.3 %reduce-scatter.21.cloned.1.call-start = ((), (), s32[]{:S(2)}) async-start(), calls=%async_computation.14 | async-start | bytes 7077888 | tf_op jit(solution)/shard_map/reduce_scatter | solution.py:276
  1261.8 239.5 %reduce-scatter.25.cloned.1.call-start = ((), (), s32[]{:S(2)}) async-start(), calls=%async_computation.20 | async-start | bytes 663552 | tf_op jit(solution)/shard_map/reduce_scatter | solution.py:309
  1264.0 268.8 %reduce-scatter.31.cloned.1.call-start = ((), (), s32[]{:S(2)}) async-start(), calls=%async_computation.23 | async-start | bytes 663552
  1264.9 7.9 copy-start.71
  1264.9 7.9 copy-start.92
  1266.0 311.9 %all-reduce.27.cloned.1.call-start = ((), (), s32[]{:S(2)}) async-start(), calls=%async_computation.27 | async-start | bytes 589824 | tf_op jit(solution)/shard_map/psum | solution.py:331
  1277.4 339.7 %reduce-scatter.35.cloned.1.call-start = ((), (), s32[]{:S(2)}) async-start(), calls=%async_computation.25 | async-start | bytes 663552
  1279.4 57.2 %copy-start.14 = (f32[512,384]{0,1:T(8,128)S(1)}, f32[512,384]{0,1:T(8,128)}, u32[]{:S(2)}) copy-start(f32[512,384]{0,1:T(8,128)} %copy-done.13) | copy-start | bytes 2359300
  1279.4 57.2 %copy-start.63 = (f32[512]{0:T(512)S(1)}, f32[512]{0:T(512)}, u32[]{:S(2)}) copy-start(f32[512]{0:T(512)} %copy-done.62) | copy-start | bytes 6148
  1331.3 7.5 copy-start.65
  1335.8 307.1 %reduce-scatter.33.cloned.1.call-start = ((), (), s32[]{:S(2)}) async-start(), calls=%async_computation.24 | async-start | bytes 663552
  1400.3 74.3 %copy-start.76 = (f32[3,128]{1,0:T(4,128)S(1)}, f32[3,128]{1,0:T(4,128)}, u32[]{:S(2)}) copy-start(f32[3,128]{1,0:T(4,128)} %convert_reduce_fusion.11) | copy-start | bytes 4612
  1400.3 74.2 %copy-start.79 = (f32[3,128]{1,0:T(4,128)S(1)}, f32[3,128]{1,0:T(4,128)}, u32[]{:S(2)}) copy-start(f32[3,128]{1,0:T(4,128)} %convert_reduce_fusion.10) | copy-start | bytes 4612
  1470.7 110.6 %copy-start.77 = (f32[3,128]{1,0:T(4,128)S(1)}, f32[3,128]{1,0:T(4,128)}, u32[]{:S(2)}) copy-start(f32[3,128]{1,0:T(4,128)} %get-tuple-element.596) | copy-start | bytes 4612
  1470.7 110.6 %copy-start.78 = (f32[3,128]{1,0:T(4,128)S(1)}, f32[3,128]{1,0:T(4,128)}, u32[]{:S(2)}) copy-start(f32[3,128]{1,0:T(4,128)} %get-tuple-element.594) | copy-start | bytes 4612
  1470.7 110.6 %copy-start.84 = (f32[384]{0:T(512)S(1)}, f32[384]{0:T(512)}, u32[]{:S(2)}) copy-start(f32[384]{0:T(512)} %add.453) | copy-start | bytes 4612
  1470.7 110.6 %copy-start.85 = (f32[384]{0:T(512)S(1)}, f32[384]{0:T(512)}, u32[]{:S(2)}) copy-start(f32[384]{0:T(512)} %add.451) | copy-start | bytes 4612
  1470.7 110.6 %copy-start.86 = (f32[384]{0:T(512)S(1)}, f32[384]{0:T(512)}, u32[]{:S(2)}) copy-start(f32[384]{0:T(512)} %add.450) | copy-start | bytes 4612
  1470.7 110.6 %copy-start.87 = (f32[384]{0:T(512)S(1)}, f32[384]{0:T(512)}, u32[]{:S(2)}) copy-start(f32[384]{0:T(512)} %add.447) | copy-start | bytes 4612
  1470.7 110.6 %copy-start.88 = (f32[384]{0:T(512)S(1)}, f32[384]{0:T(512)}, u32[]{:S(2)}) copy-start(f32[384]{0:T(512)} %add.449) | copy-start | bytes 4612
  1470.7 110.6 %copy-start.89 = (f32[384]{0:T(512)S(1)}, f32[384]{0:T(512)}, u32[]{:S(2)}) copy-start(f32[384]{0:T(512)} %add.452) | copy-start | bytes 4612
  1470.8 144.0 %copy-start.9 = (bf16[384,384]{1,0:T(8,128)(2,1)S(1)}, bf16[384,384]{1,0:T(8,128)(2,1)}, u32[]{:S(2)}) copy-start(bf16[384,384]{1,0:T(8,128)(2,1)} %copy-done.8) | copy-start | bytes 884740
  1471.1 145.2 %copy-start.33 = (bf16[384,384]{1,0:T(8,128)(2,1)S(1)}, bf16[384,384]{1,0:T(8,128)(2,1)}, u32[]{:S(2)}) copy-start(bf16[384,384]{1,0:T(8,128)(2,1)} %copy-done.32) | copy-start | bytes 884740
  1474.5 221.2 %all-reduce.25.cloned.1.call-start = ((), (), s32[]{:S(2)}) async-start(), calls=%async_computation.26 | async-start | bytes 672768 | tf_op jit(solution)/shard_map/psum | solution.py:327
  1614.8 29.8 %copy-start.26 = (bf16[3,1,512,128]{2,3,1,0:T(8,128)(2,1)S(1)}, bf16[3,1,512,128]{2,3,1,0:T(8,128)(2,1)}, u32[]{:S(2)}) copy-start(bf16[3,1,512,128]{2,3,1,0:T(8,128)(2,1)} %copy-done.25) | copy-start | bytes 1179652
  1614.8 29.8 %copy-start.34 = (bf16[384,384]{1,0:T(8,128)(2,1)S(1)}, bf16[384,384]{1,0:T(8,128)(2,1)}, u32[]{:S(2)}) copy-start(bf16[384,384]{1,0:T(8,128)(2,1)} %copy-done.32) | copy-start | bytes 884740
  (64 other events, 228.2 us)
Sparse Core Ops, SparseCore 0:
  64.6 37.3 all-gather.14
  103.6 39.9 all-gather.16
  145.8 37.1 all-gather.18
  184.5 21.5 all-gather.10
  207.5 22.4 all-gather.12
  231.5 38.0 all-gather.20
  512.7 34.4 reduce-scatter.28
  549.5 35.4 reduce-scatter.26
  894.1 68.0 reduce-scatter.18
  1260.5 68.1 reduce-scatter.22
  1331.0 68.0 reduce-scatter.16
  1401.3 68.1 reduce-scatter.20
  1471.8 29.4 reduce-scatter.24
  1503.4 29.3 reduce-scatter.30
  1536.2 41.7 all-reduce.26
  1580.2 31.1 reduce-scatter.34
  1613.6 29.3 reduce-scatter.32
  1649.5 46.1 all-reduce.24
where the time goes:
time: 1730 us; the launch traced here: 1720 us
  matrix products  697 us (40%)
  waiting for transfers between devices  353 us (20%)
  other arithmetic  321 us (19%)
  local copies, waits for them, and re-layouts  174 us (10%)
  blocking collectives  133 us (8%)
  loops' own time  21.4 us (1%)
  between operations  18.4 us (1%)
    convert_element_type x6, other arithmetic, group_backward(): grad_scores = (attn_weights * (grad_weights - centre)).astype(jnp.bfloat16)  166 us
    dot_general x12, matrix products, masked_scores(): jnp.einsum('bqhd,bkhd->bhqk', query_group, key_group, preferred_element_t...  165 us
    dot_general x6, matrix products, group_backward(): jnp.einsum('bqhd,bkhd->bhqk', grad_context, value_group, preferred_elemen...  148 us
    reduce_scatter x2, waiting for transfers between devices, on_device(): lax.psum_scatter(key_groups, 'grp', scatter_dimension=2, tiled=True)  128 us
    dot_general x6, matrix products, group_backward(): jnp.einsum('bhqk,bqhd->bkhd', weights_low, grad_context, preferred_elemen...  97.6 us
    reduce_sum x6, other arithmetic, group_forward(): jnp.sum(jnp.exp(scores - highest), axis=-1, keepdims=True)  90.9 us
    dot_general x6, matrix products, group_forward(): jnp.einsum('bhqk,bkhd->bqhd', weights_low, value_group, preferred_element...  90.2 us
    dot_general x6, matrix products, group_backward(): jnp.einsum('bhqk,bkhd->bqhd', grad_scores, key_group, preferred_element_t...  65.4 us
  transfers between devices with their start and end apart: 18, of which 8 were waited for; matrix products, arithmetic and copies ran while one was open for 57% of the time, Pallas kernels for 0%

commit v1 on v0

--- a/solution.py
+++ b/solution.py
@@ -3,6 +3,8 @@
 import jax
 import jax.numpy as jnp
 from jax import lax
+from jax.experimental import pallas as pl
+from jax.experimental.pallas import tpu as pltpu
 from jax.sharding import PartitionSpec as P
 
 H = 12
@@ -361,6 +363,971 @@
     )
 
 
+HEAD = 32
+LANES = 128
+QB = 256
+KB = 256
+AWAY = 2.0 ** 100
+MESH = pl.DeviceIdType.MESH
+BIG = 100 * 1024 * 1024 // 2
+LOG2E = 1.4426950408889634
+
+
+def halves(value):
+    first = value.astype(jnp.bfloat16).astype(jnp.float32)
+    rest = value - first
+    second = rest.astype(jnp.bfloat16).astype(jnp.float32)
+    third = (rest - second).astype(jnp.bfloat16).astype(jnp.float32)
+    return first, second, third
+
+
+def dot(left, right):
+    return jnp.dot(left, right, preferred_element_type=jnp.float32)
+
+
+def iota(shape, dim):
+    return lax.broadcasted_iota(jnp.int32, shape, dim)
+
+
+def where_am_i():
+    r = lax.axis_index("rep")
+    g = lax.axis_index("grp")
+    return r, g, lax.div(g, 2), lax.rem(g, 2)
+
+
+def remote(src, dst, send, recv, r, g):
+    return pltpu.make_async_remote_copy(
+        src_ref=src, dst_ref=dst, send_sem=send, recv_sem=recv, device_id=(r, g), device_id_type=MESH
+    )
+
+
+def greet(r, g, reps, group):
+    barrier = pltpu.get_barrier_semaphore()
+    for d in range(1, group):
+        pl.semaphore_signal(barrier, inc=1, device_id=(r, lax.rem(g + d, group)), device_id_type=MESH)
+    for d in range(1, reps):
+        pl.semaphore_signal(barrier, inc=1, device_id=(lax.rem(r + d, reps), g), device_id_type=MESH)
+    pl.semaphore_wait(barrier, group + reps - 2)
+
+
+def gather_kernel(
+    tok, wp, small, x_out, w_out, s_out,
+    lsem, tsend, trecv, psend, wsend1, wrecv1, wsend2, wrecv2, wsend3, wrecv3, ssend, srecv,
+):
+    r, g, z, c = where_am_i()
+    reps, chips = 4, 4
+    p = 2 * z + 1 - c
+    greet(r, g, reps, 2 * chips)
+    own_w = pltpu.make_async_copy(wp.at[r], w_out.at[r, c, z], lsem.at[1])
+    own_w.start()
+    own_x = pltpu.make_async_copy(tok.at[c], x_out.at[g], lsem.at[0])
+    own_x.start()
+    own_s = pltpu.make_async_copy(small, s_out.at[g], lsem.at[2])
+    own_s.start()
+    swap = remote(tok.at[1 - c], x_out.at[g], psend, trecv.at[g], r, p)
+    swap.start()
+
+    first = []
+    for d in range(1, chips):
+        zz = lax.rem(z + d, chips)
+        copy = remote(wp.at[r], w_out.at[r, c, z], wsend1.at[d - 1], wrecv1.at[z], r, 2 * zz + c)
+        copy.start()
+        first.append(copy)
+    smalls = []
+    for d in range(1, 2 * chips):
+        copy = remote(small, s_out.at[g], ssend.at[d - 1], srecv.at[g], r, lax.rem(g + d, 2 * chips))
+        copy.start()
+        smalls.append(copy)
+
+    def pass_on(b, src, way):
+        to = g + 2 if way == 0 else g - 2
+        return remote(src, x_out.at[b], tsend.at[way, b], trecv.at[b], r, to)
+
+    def forward(b, src, way):
+        ok = z < chips - 1 if way == 0 else z > 0
+
+        @pl.when(ok)
+        def _():
+            pass_on(b, src, way).start()
+
+    def arrived(b):
+        remote(x_out.at[b], x_out.at[b], tsend.at[0, b], trecv.at[b], r, p).wait_recv()
+
+    forward(g, tok.at[c], 0)
+    forward(g, tok.at[c], 1)
+    arrived(p)
+    forward(p, x_out.at[p], 0)
+    forward(p, x_out.at[p], 1)
+
+    def tokens_from(d):
+        for k in range(2):
+            @pl.when(z >= d)
+            def _():
+                b = 2 * (z - d) + (c if k == 0 else 1 - c)
+                arrived(b)
+                forward(b, x_out.at[b], 0)
+
+            @pl.when(z + d < chips)
+            def _():
+                b = 2 * (z + d) + (c if k == 0 else 1 - c)
+                arrived(b)
+                forward(b, x_out.at[b], 1)
+
+    tokens_from(1)
+    own_w.wait()
+    for d in range(1, chips):
+        zz = lax.rem(z + d, chips)
+        remote(wp.at[r], w_out.at[r, c, zz], wsend1.at[0], wrecv1.at[zz], r, g).wait_recv()
+    second = []
+    for d in range(1, reps):
+        copy = remote(
+            w_out.at[r, c], w_out.at[r, c], wsend2.at[d - 1], wrecv2.at[r], lax.rem(r + d, reps), g
+        )
+        copy.start()
+        second.append(copy)
+    third = [remote(w_out.at[r, c], w_out.at[r, c], wsend3.at[r], wrecv3.at[r], r, p)]
+    third[0].start()
+    tokens_from(2)
+    for d in range(1, reps):
+        q = lax.rem(r + d, reps)
+        remote(w_out.at[q, c], w_out.at[q, c], wsend2.at[0], wrecv2.at[q], r, p).wait_recv()
+        copy = remote(w_out.at[q, c], w_out.at[q, c], wsend3.at[q], wrecv3.at[q], r, p)
+        copy.start()
+        third.append(copy)
+    tokens_from(3)
+    for q in range(reps):
+        remote(w_out.at[q, 1 - c], w_out.at[q, 1 - c], wsend3.at[q], wrecv3.at[q], r, p).wait_recv()
+    for d in range(1, 2 * chips):
+        b = lax.rem(g + d, 2 * chips)
+        remote(small, s_out.at[b], ssend.at[0], srecv.at[b], r, p).wait_recv()
+    own_x.wait()
+    own_s.wait()
+    swap.wait_send()
+    for copy in first + smalls + second + third:
+        copy.wait_send()
+    for b in range(2 * chips):
+        @pl.when((z < chips - 1) & (b < 2 * z + 2))
+        def _():
+            pass_on(b, x_out.at[b], 0).wait_send()
+
+        @pl.when((z > 0) & (b >= 2 * z))
+        def _():
+            pass_on(b, x_out.at[b], 1).wait_send()
+
+
+def gather(tokens, wp, small):
+    dma = pltpu.SemaphoreType.DMA
+    anywhere = pl.BlockSpec(memory_space=pl.ANY)
+    rows, width = tokens.shape[1:]
+    return pl.pallas_call(
+        gather_kernel,
+        name="gather",
+        out_shape=(
+            jax.ShapeDtypeStruct((8, rows, width), jnp.bfloat16),
+            jax.ShapeDtypeStruct((4, 2, 4) + wp.shape[1:], jnp.bfloat16),
+            jax.ShapeDtypeStruct((8,) + small.shape, jnp.bfloat16),
+        ),
+        in_specs=[anywhere] * 3,
+        out_specs=[anywhere] * 3,
+        scratch_shapes=[
+            dma((3,)), dma((2, 8)), dma((8,)), dma, dma((3,)), dma((4,)), dma((3,)), dma((4,)),
+            dma((4,)), dma((4,)), dma((7,)), dma((8,)),
+        ],
+        compiler_params=pltpu.CompilerParams(collective_id=1, has_side_effects=True),
+    )(tokens, wp, small)
+
+
+def span_of(starts, q0, docs):
+    low = jnp.int32(0)
+    high = starts[docs]
+    for d in range(docs):
+        low = jnp.where(starts[d] <= q0, jnp.maximum(low, starts[d]), low)
+        high = jnp.where(starts[d + 1] >= q0 + QB, jnp.minimum(high, starts[d + 1]), high)
+    first = lax.div(low, LANES)
+    last = lax.div(high + LANES - 1, LANES)
+    steps = lax.div(last - first + KB // LANES - 1, KB // LANES)
+    total = lax.div(starts[docs], LANES)
+    first = jnp.minimum(first, total - steps * (KB // LANES))
+    return first, steps
+
+
+def attend_kernel(
+    place, x, w, bias, seg, kv, qt, kt, qr, ctx, ctx32, spans, wrow, wtr, vt, acc, starts,
+):
+    heads = kv.shape[0]
+    length, width = x.shape
+    blocks, hw, rows = ctx.shape
+    docs = 8
+    z = place[0]
+    c = place[1]
+    span = heads * HEAD
+
+    full = [
+        jnp.concatenate([w[g % 2, g // 2, 48 * i : 48 * i + 48, :] for g in range(8)], axis=0)
+        for i in range(3)
+    ]
+    lane = iota((width, heads * LANES), 1)
+    head, inner = lax.div(lane, LANES), lax.rem(lane, LANES)
+    column = span * z + head * HEAD + lax.rem(inner, HEAD)
+    hit = iota((width, heads * LANES), 0) == column
+    pick_k = jnp.where(hit & (inner < 64), 1.0, 0.0).astype(jnp.bfloat16)
+    pick_v = jnp.where(hit & (inner >= 64) & (inner < 96), 1.0, 0.0).astype(jnp.bfloat16)
+    pick_q = jnp.where(hit & (inner >= 32) & (inner < 64), 1.0, 0.0).astype(jnp.bfloat16)
+    wrow[0] = (dot(full[1], pick_k) + dot(full[2], pick_v)).astype(jnp.bfloat16)
+    wrow[1] = dot(full[0], pick_q).astype(jnp.bfloat16)
+    row_kv = dot(bias[1:2, :], pick_v)
+    row_q = dot(bias[0:1, :], pick_q)
+    pick_t = jnp.where(
+        iota((span, width), 1) == span * z + iota((span, width), 0), 1.0, 0.0
+    ).astype(jnp.bfloat16)
+    for i in range(3):
+        wtr[i] = lax.dot_general(
+            pick_t, full[i], (((1,), (1,)), ((), ())), preferred_element_type=jnp.float32
+        ).astype(jnp.bfloat16)
+    column_bias = lax.dot_general(
+        pick_t, bias[...], (((1,), (1,)), ((), ())), preferred_element_type=jnp.float32
+    )
+    col_q, col_v = column_bias[:, 0:1], column_bias[:, 1:2]
+
+    ids = seg[...]
+    starts[0] = jnp.int32(0)
+    for d in range(1, docs):
+        starts[d] = jnp.sum(jnp.where(ids < d, 1.0, 0.0)).astype(jnp.int32)
+    starts[docs] = jnp.int32(length)
+
+    scale = (HEAD ** -0.5) * LOG2E
+    one_lane = lax.rem(iota((1, heads * LANES), 1), LANES)
+    ones_row = jnp.where((one_lane >= 104) & (one_lane < 107), 1.0, 0.0)
+
+    def project(b, carry):
+        r0 = pl.multiple_of(b * rows, rows)
+        xb = x[pl.ds(r0, rows), :]
+        idrow = seg[pl.ds(b, 1), :]
+        same = jnp.where(iota((8, rows), 0) == idrow, 1.0, 0.0)
+        hot = jnp.concatenate(
+            [jnp.zeros((96, rows), jnp.float32), same, jnp.zeros((24, rows), jnp.float32)], axis=0
+        ).T
+        flat = dot(xb, wrow[0]) + (row_kv + ones_row)
+        for h in range(heads):
+            kv[h, pl.ds(r0, rows), :] = (flat[:, h * LANES : (h + 1) * LANES] + hot).astype(
+                jnp.bfloat16
+            )
+        flat = (dot(xb, wrow[1]) + row_q).astype(jnp.bfloat16)
+        for h in range(heads):
+            qr[h, pl.ds(r0, rows), :] = flat[:, h * LANES : (h + 1) * LANES]
+
+        def turned(i):
+            return lax.dot_general(
+                wtr[i], xb, (((1,), (1,)), ((), ())), preferred_element_type=jnp.float32
+            )
+
+        q_t = (turned(0) + col_q).astype(jnp.bfloat16).astype(jnp.float32) * scale
+        q_hi = q_t.astype(jnp.bfloat16)
+        q_lo = (q_t - q_hi.astype(jnp.float32)).astype(jnp.bfloat16)
+        k_t = turned(1).astype(jnp.bfloat16)
+        v_t = (turned(2) + col_v).astype(jnp.bfloat16)
+        far = jnp.concatenate([(same - 1.0) * AWAY, jnp.zeros((8, rows), jnp.float32)], axis=0)
+        far = far.astype(jnp.bfloat16)
+        one = jnp.where(iota((16, rows), 0) == 0, 1.0, 0.0).astype(jnp.bfloat16)
+        cols = pl.ds(r0, rows)
+        for h in range(heads):
+            part = slice(h * HEAD, (h + 1) * HEAD)
+            qt[h, 0:32, cols] = q_hi[part]
+            qt[h, 32:64, cols] = q_lo[part]
+            qt[h, 64:96, cols] = jnp.zeros((32, rows), jnp.bfloat16)
+            qt[h, 96:112, cols] = far
+            qt[h, 112:128, cols] = jnp.zeros((16, rows), jnp.bfloat16)
+            kt[h, :, cols] = k_t[part]
+            vt[h, 0:32, cols] = v_t[part]
+            vt[h, 32:48, cols] = one
+        return carry
+
+    lax.fori_loop(0, blocks, project, 0)
+
+    per = rows // QB
+
+    def query_block(b, carry):
+        q0 = pl.multiple_of(b * QB, QB)
+        first, steps = span_of(starts, q0, docs)
+        spans[0, b] = first
+        spans[1, b] = steps
+        acc[...] = jnp.zeros_like(acc)
+
+        def key_block(i, tops):
+            k0 = pl.multiple_of((first + i * (KB // LANES)) * LANES, LANES)
+            new = []
+            for h in range(heads):
+                s = dot(kv[h, pl.ds(k0, KB), :], qt[h, :, pl.ds(q0, QB)])
+                top = jnp.maximum(tops[h], jnp.max(s, axis=0, keepdims=True))
+                p = jnp.exp2(s - top).astype(jnp.bfloat16)
+                acc[h] = acc[h] * jnp.exp2(tops[h] - top) + dot(vt[h, :, pl.ds(k0, KB)], p)
+                new.append(top)
+            return tuple(new)
+
+        lowest = jnp.full((1, QB), -3e38, jnp.float32)
+        tops = lax.fori_loop(0, steps, key_block, (lowest,) * heads)
+        g = lax.div(b, per)
+        off = pl.multiple_of(lax.rem(b, per) * QB, QB)
+        same = jnp.where(iota((8, QB), 0) == seg[pl.ds(g, 1), pl.ds(off, QB)], 1.0, 0.0)
+        for h in range(heads):
+            total = acc[h, 32:33, :]
+            out = acc[h, 0:32, :] / total
+            ctx[g, h * HEAD : (h + 1) * HEAD, pl.ds(off, QB)] = out.astype(jnp.bfloat16)
+            ctx32[g, h * HEAD : (h + 1) * HEAD, pl.ds(off, QB)] = out
+            parts = halves(-(tops[h] + jnp.log2(total)))
+            tail = jnp.concatenate(
+                [(same - 1.0) * AWAY, *parts, jnp.zeros((5, QB), jnp.float32)], axis=0
+            )
+            qt[h, 96:112, pl.ds(q0, QB)] = tail.astype(jnp.bfloat16)
+        return carry
+
+    lax.fori_loop(0, length // QB, query_block, 0)
+
+
+def attend(place, x, w, bias, seg):
+    blocks, rows, width = x.shape
+    length = blocks * rows
+    heads = 3
+    vm = pl.BlockSpec(memory_space=pltpu.VMEM)
+    sm = pl.BlockSpec(memory_space=pltpu.SMEM)
+    bf, f4 = jnp.bfloat16, jnp.float32
+    return pl.pallas_call(
+        attend_kernel,
+        name="attend",
+        out_shape=(
+            jax.ShapeDtypeStruct((heads, length, LANES), bf),
+            jax.ShapeDtypeStruct((heads, LANES, length), bf),
+            jax.ShapeDtypeStruct((heads, HEAD, length), bf),
+            jax.ShapeDtypeStruct((heads, length, LANES), bf),
+            jax.ShapeDtypeStruct((blocks, heads * HEAD, rows), bf),
+            jax.ShapeDtypeStruct((blocks, heads * HEAD, rows), f4),
+            jax.ShapeDtypeStruct((2, length // QB), jnp.int32),
+        ),
+        in_specs=[sm, vm, vm, vm, vm],
+        out_specs=[vm] * 6 + [sm],
+        scratch_shapes=[
+            pltpu.VMEM((2, width, heads * LANES), bf),
+            pltpu.VMEM((3, heads * HEAD, width), bf),
+            pltpu.VMEM((heads, 48, length), bf),
+            pltpu.VMEM((heads, 48, QB), f4),
+            pltpu.SMEM((16,), jnp.int32),
+        ],
+        compiler_params=pltpu.CompilerParams(vmem_limit_bytes=BIG),
+    )(place, x.reshape(length, width), w, bias, seg)
+
+
+def context_kernel(src, dst, lsem, send, recv):
+    r, g, z, c = where_am_i()
+    greet(r, g, 1, 8)
+    own = pltpu.make_async_copy(src.at[g], dst.at[c, z], lsem)
+    own.start()
+    copies = []
+    for d in range(1, 8):
+        to = lax.rem(g + d, 8)
+        copy = remote(src.at[to], dst.at[c, z], send.at[d - 1], recv.at[g], r, to)
+        copy.start()
+        copies.append(copy)
+    for d in range(1, 8):
+        b = lax.rem(g + d, 8)
+        remote(src.at[g], dst.at[lax.rem(b, 2), lax.div(b, 2)], send.at[0], recv.at[b], r, b).wait_recv()
+    for copy in copies:
+        copy.wait_send()
+    own.wait()
+
+
+def exchange_context(ctx):
+    dma = pltpu.SemaphoreType.DMA
+    anywhere = pl.BlockSpec(memory_space=pl.ANY)
+    return pl.pallas_call(
+        context_kernel,
+        name="exchange_context",
+        out_shape=jax.ShapeDtypeStruct((2, 4) + ctx.shape[1:], ctx.dtype),
+        in_specs=[anywhere],
+        out_specs=anywhere,
+        scratch_shapes=[dma, dma((7,)), dma((8,))],
+        compiler_params=pltpu.CompilerParams(collective_id=2, has_side_effects=True),
+    )(ctx)
+
+
+def cotangent_kernel(src, pg, dst, pg_out, lsem, send, recv, psend, precv):
+    r, g, z, c = where_am_i()
+    greet(r, g, 1, 8)
+    pair = remote(pg.at[1 - c], pg_out, psend, precv, r, 2 * z + 1 - c)
+    pair.start()
+    own = pltpu.make_async_copy(src.at[c, z], dst.at[g], lsem)
+    own.start()
+    copies = []
+    for d in range(1, 8):
+        to = lax.rem(g + d, 8)
+        copy = remote(
+            src.at[lax.rem(to, 2), lax.div(to, 2)], dst.at[g], send.at[d - 1], recv.at[g], r, to
+        )
+        copy.start()
+        copies.append(copy)
+    for d in range(1, 8):
+        b = lax.rem(g + d, 8)
+        remote(src.at[c, z], dst.at[b], send.at[0], recv.at[b], r, b).wait_recv()
+    for copy in copies:
+        copy.wait_send()
+    pair.wait()
+    own.wait()
+
+
+def exchange_cotangent(src, pg):
+    dma = pltpu.SemaphoreType.DMA
+    anywhere = pl.BlockSpec(memory_space=pl.ANY)
+    return pl.pallas_call(
+        cotangent_kernel,
+        name="exchange_cotangent",
+        out_shape=(
+            jax.ShapeDtypeStruct((8,) + src.shape[2:], src.dtype),
+            jax.ShapeDtypeStruct(pg.shape[1:], pg.dtype),
+        ),
+        in_specs=[anywhere] * 2,
+        out_specs=[anywhere] * 2,
+        scratch_shapes=[dma, dma((7,)), dma((8,)), dma, dma],
+        compiler_params=pltpu.CompilerParams(collective_id=3, has_side_effects=True),
+    )(src, pg)
+
+
+def dense_kernel(
+    tok, og, ctx, w, vec, inner_bias,
+    layer_out, grad_one_out, gctx, pg, wo, wi, wu, gwo, gwi, gwu, sums, inner_sum,
+):
+    seqs, rows, width = tok.shape
+    slabs = wi.shape[0]
+    block = 256
+    per = rows // block
+    for g in range(8):
+        c, z = g % 2, g // 2
+        wo[48 * g : 48 * g + 48, :] = w[1, c, z, 0:48, :]
+        wi[0, 48 * g : 48 * g + 48, :] = w[1, c, z, 48:96, :]
+        wi[1, 48 * g : 48 * g + 48, :] = w[1, c, z, 96:144, :]
+        wi[2, 48 * g : 48 * g + 48, :] = w[2, c, z, 0:48, :]
+        wi[3, 48 * g : 48 * g + 48, :] = w[2, c, z, 48:96, :]
+        wu[g // 2, 192 * c : 192 * c + 48, :] = w[2, c, z, 96:144, :]
+        wu[g // 2, 192 * c + 48 : 192 * c + 192, :] = w[3, c, z, :, :]
+    for ref in (gwo, gwi, gwu, sums, inner_sum):
+        ref[...] = jnp.zeros_like(ref)
+
+    out_bias, outer_bias = vec[2:3, :], vec[3:4, :]
+    gain_one, shift_one = vec[4:5, :], vec[5:6, :]
+    gain_two, shift_two = vec[6:7, :], vec[7:8, :]
+
+    def normal(value):
+        centre = value - jnp.mean(value, axis=-1, keepdims=True)
+        rate = lax.rsqrt(jnp.mean(centre * centre, axis=-1, keepdims=True) + norm_epsilon)
+        return centre * rate, rate
+
+    def normal_back(grad, gain, n, rate):
+        u = grad * gain
+        return rate * (
+            u - jnp.mean(u, axis=-1, keepdims=True) - n * jnp.mean(u * n, axis=-1, keepdims=True)
+        )
+
+    def total(value):
+        return jnp.sum(value, axis=0, keepdims=True)
+
+    def turn_dot(left, right):
+        return lax.dot_general(
+            left, right, (((0,), (0,)), ((), ())), preferred_element_type=jnp.float32
+        )
+
+    def dot_turn(left, right):
+        return lax.dot_general(
+            left, right, (((1,), (1,)), ((), ())), preferred_element_type=jnp.float32
+        )
+
+    def one(b, carry):
+        s = lax.div(b, per)
+        r0 = pl.multiple_of(lax.rem(b, per) * block, block)
+        here = pl.ds(r0, block)
+        ctx_t = ctx[s, :, here]
+        context = ctx_t.astype(jnp.float32).T.astype(jnp.bfloat16)
+        x = tok[s, here, :].astype(jnp.float32)
+        n_one, rate_one = normal(x + (dot(context, wo[...]) + out_bias))
+        hidden = n_one * gain_one + shift_one
+        low = hidden.astype(jnp.bfloat16)
+        low_t = hidden.T.astype(jnp.bfloat16)
+        feed = jnp.zeros((block, width), jnp.float32)
+        slopes, actives = [], []
+        for j in range(slabs):
+            inner = dot(low, wi[j]) + inner_bias[:, j * width : (j + 1) * width]
+            cdf = 0.5 + 0.5 * lax.erf(inner * (0.5 ** 0.5))
+            pdf = jnp.exp(inner * inner * -0.5) * 0.3989422804014327
+            slopes.append(cdf + inner * pdf)
+            active = inner * cdf
+            actives.append(active)
+            feed = feed + dot(active.astype(jnp.bfloat16), wu[j])
+        n_two, rate_two = normal(hidden + (feed + outer_bias))
+        layer_out[s, here, :] = (n_two * gain_two + shift_two).astype(jnp.bfloat16)
+        grad = og[s, here, :].astype(jnp.float32)
+        grad_two = normal_back(grad, gain_two, n_two, rate_two)
+        grad_feed = grad_two.astype(jnp.bfloat16)
+        grad_hidden = grad_two
+        for j in range(slabs):
+            grad_inner = (dot_turn(grad_feed, wu[j]) * slopes[j]).astype(jnp.bfloat16)
+            inner_sum[:, j * width : (j + 1) * width] += total(grad_inner.astype(jnp.float32))
+            grad_hidden = grad_hidden + dot_turn(grad_inner, wi[j])
+            gwi[j] += dot(low_t, grad_inner)
+            gwu[j] += dot(actives[j].T.astype(jnp.bfloat16), grad_feed)
+        grad_one = normal_back(grad_hidden, gain_one, n_one, rate_one)
+        grad_one_out[s, here, :] = grad_one
+        grad_att = grad_one.astype(jnp.bfloat16)
+        gctx[s, :, here] = dot_turn(wo[...], grad_att).astype(jnp.bfloat16)
+        gwo[...] += dot(ctx_t, grad_att)
+        sums[0:1, :] += total(grad_att.astype(jnp.float32))
+        sums[1:2, :] += total(grad_feed.astype(jnp.float32))
+        sums[2:3, :] += total(grad_hidden * n_one)
+        sums[3:4, :] += total(grad_hidden)
+        sums[4:5, :] += total(grad * n_two)
+        sums[5:6, :] += total(grad)
+        return carry
+
+    lax.fori_loop(0, seqs * per, one, 0)
+    for g in range(8):
+        c, z = g % 2, g // 2
+        mine = slice(48 * g, 48 * g + 48)
+        pg[c, 0, z, 0:48, :] = gwo[mine, :].astype(jnp.bfloat16)
+        pg[c, 0, z, 48:96, :] = gwi[0, mine, :].astype(jnp.bfloat16)
+        pg[c, 1, z, 0:48, :] = gwi[1, mine, :].astype(jnp.bfloat16)
+        pg[c, 1, z, 48:96, :] = gwi[2, mine, :].astype(jnp.bfloat16)
+        pg[c, 2, z, 0:48, :] = gwi[3, mine, :].astype(jnp.bfloat16)
+        base = 192 * c
+        pg[c, 0, z, 96:112, :] = gwu[z, base : base + 16, :].astype(jnp.bfloat16)
+        pg[c, 1, z, 96:112, :] = gwu[z, base + 16 : base + 32, :].astype(jnp.bfloat16)
+        pg[c, 2, z, 48:112, :] = gwu[z, base + 32 : base + 96, :].astype(jnp.bfloat16)
+        pg[c, 3, z, 0:96, :] = gwu[z, base + 96 : base + 192, :].astype(jnp.bfloat16)
+        pg[c, 3, z, 96:112, :] = jnp.concatenate(
+            [sums[...]]
+            + [inner_sum[:, j * width : (j + 1) * width] for j in range(slabs)]
+            + [jnp.zeros((6, width), jnp.float32)],
+            axis=0,
+        ).astype(jnp.bfloat16)
+
+
+def dense(tok, og, ctx, w, vec, inner_bias):
+    seqs, rows, width = tok.shape
+    vm = pl.BlockSpec(memory_space=pltpu.VMEM)
+    bf, f4 = jnp.bfloat16, jnp.float32
+    return pl.pallas_call(
+        dense_kernel,
+        name="dense",
+        out_shape=(
+            jax.ShapeDtypeStruct((seqs, rows, width), bf),
+            jax.ShapeDtypeStruct((seqs, rows, width), f4),
+            jax.ShapeDtypeStruct((seqs, width, rows), bf),
+            jax.ShapeDtypeStruct((2, 4, 4, 112, width), bf),
+        ),
+        in_specs=[vm] * 6,
+        out_specs=[vm] * 4,
+        scratch_shapes=[
+            pltpu.VMEM((width, width), bf),
+            pltpu.VMEM((4, width, width), bf),
+            pltpu.VMEM((4, width, width), bf),
+            pltpu.VMEM((width, width), f4),
+            pltpu.VMEM((4, width, width), f4),
+            pltpu.VMEM((4, width, width), f4),
+            pltpu.VMEM((6, width), f4),
+            pltpu.VMEM((1, 4 * width), f4),
+        ],
+        compiler_params=pltpu.CompilerParams(vmem_limit_bytes=BIG),
+    )(tok, og, ctx, w, vec, inner_bias)
+
+
+def attend_back_kernel(
+    place, spans, x, kv, qt, kt, qr, gctx, ctx32, pg, pg_in, out, gq, pr, dt, do, acc, dq,
+):
+    heads = kv.shape[0]
+    length, width = x.shape
+    blocks, _, rows = gctx.shape
+    z = place[0]
+    c = place[1]
+    scale = HEAD ** -0.5
+
+    def prepare(g, carry):
+        r0 = pl.multiple_of(g * rows, rows)
+        cols = pl.ds(r0, rows)
+        for h in range(heads):
+            part = slice(h * HEAD, (h + 1) * HEAD)
+            grad = gctx[g, part, :]
+            wide = grad.astype(jnp.float32)
+            delta = -jnp.sum(wide * ctx32[g, part, :], axis=0, keepdims=True)
+            dt[h, 0:64, cols] = jnp.zeros((64, rows), jnp.bfloat16)
+            dt[h, 64:96, cols] = grad
+            tail = jnp.concatenate(
+                [jnp.zeros((8, rows), jnp.float32), *halves(delta), jnp.zeros((21, rows), jnp.float32)],
+                axis=0,
+            )
+            dt[h, 96:128, cols] = tail.astype(jnp.bfloat16)
+            do[h, cols, :] = jnp.concatenate(
+                [wide, jnp.zeros((96, rows), jnp.float32)], axis=0
+            ).T.astype(jnp.bfloat16)
+        return carry
+
+    lax.fori_loop(0, blocks, prepare, 0)
+    for s in range(4):
+        pr[s] = (pg[c, s].astype(jnp.float32) + pg_in[s].astype(jnp.float32)).astype(jnp.bfloat16)
+    acc[...] = jnp.zeros_like(acc)
+    per = rows // QB
+
+    def query_block(b, carry):
+        q0 = pl.multiple_of(b * QB, QB)
+        first = spans[0, b]
+        dq[...] = jnp.zeros_like(dq)
+
+        def key_block(i, inner):
+            k0 = pl.multiple_of((first + i * (KB // LANES)) * LANES, LANES)
+            keys = pl.ds(k0, KB)
+            for h in range(heads):
+                rows_k = kv[h, keys, :]
+                p = jnp.exp2(dot(rows_k, qt[h, :, pl.ds(q0, QB)]))
+                ds = (p * dot(rows_k, dt[h, :, pl.ds(q0, QB)])).astype(jnp.bfloat16)
+                acc[h, keys, :] += dot(p.astype(jnp.bfloat16), do[h, pl.ds(q0, QB), :]) + dot(
+                    ds, qr[h, pl.ds(q0, QB), :]
+                )
+                dq[h] += dot(kt[h, :, keys], ds)
+            return inner
+
+        lax.fori_loop(0, spans[1, b], key_block, 0)
+        g = lax.div(b, per)
+        off = pl.multiple_of(lax.rem(b, per) * QB, QB)
+        for h in range(heads):
+            out[g, h * HEAD : (h + 1) * HEAD, pl.ds(off, QB)] = (dq[h] * scale).astype(jnp.bfloat16)
+        return carry
+
+    lax.fori_loop(0, length // QB, query_block, 0)
+
+    gq[...] = jnp.zeros_like(gq)
+    span = heads * HEAD
+
+    def finish(g, totals):
+        r0 = pl.multiple_of(g * rows, rows)
+        cols = pl.ds(r0, rows)
+        for h in range(heads):
+            both = acc[h, cols, :].T
+            out[g, 2 * span + h * HEAD : 2 * span + (h + 1) * HEAD, :] = both[0:32].astype(jnp.bfloat16)
+            out[g, span + h * HEAD : span + (h + 1) * HEAD, :] = (both[32:64] * scale).astype(
+                jnp.bfloat16
+            )
+        piece = out[g]
+        grad = dot(piece, x[cols, :])
+        summed = jnp.sum(piece.astype(jnp.float32), axis=1, keepdims=True)
+        return totals[0] + grad, totals[1] + summed
+
+    grads, summed = lax.fori_loop(
+        0,
+        blocks,
+        finish,
+        (jnp.zeros((3 * span, width), jnp.float32), jnp.zeros((3 * span, 1), jnp.float32)),
+    )
+    grads_t = grads.T
+    for g in range(8):
+        cc, zz = g % 2, g // 2
+        gq[cc, zz, :, 0 : 3 * span] = grads_t[48 * g : 48 * g + 48, :].astype(jnp.bfloat16)
+    for cc in range(2):
+        mine = jnp.concatenate(
+            [
+                summed[48 * cc : 48 * cc + 48, :],
+                summed[2 * span + 48 * cc : 2 * span + 48 * cc + 48, :],
+                jnp.zeros((48, 94), jnp.float32),
+            ],
+            axis=1,
+        )
+        gq[cc, z, :, 3 * span :] = mine.astype(jnp.bfloat16)
+
+
+def attend_back(place, spans, x, kv, qt, kt, qr, gctx, ctx32, pg, pg_in):
+    blocks, rows, width = x.shape
+    length = blocks * rows
+    heads = kv.shape[0]
+    vm = pl.BlockSpec(memory_space=pltpu.VMEM)
+    sm = pl.BlockSpec(memory_space=pltpu.SMEM)
+    bf, f4 = jnp.bfloat16, jnp.float32
+    return pl.pallas_call(
+        attend_back_kernel,
+        name="attend_back",
+        out_shape=(
+            jax.ShapeDtypeStruct((blocks, 3 * heads * HEAD, rows), bf),
+            jax.ShapeDtypeStruct((2, 4, 48, width), bf),
+            jax.ShapeDtypeStruct(pg_in.shape, bf),
+        ),
+        in_specs=[sm, sm] + [vm] * 9,
+        out_specs=[vm] * 3,
+        scratch_shapes=[
+            pltpu.VMEM((heads, LANES, length), bf),
+            pltpu.VMEM((heads, length, LANES), bf),
+            pltpu.VMEM((heads, length, LANES), f4),
+            pltpu.VMEM((heads, HEAD, QB), f4),
+        ],
+        compiler_params=pltpu.CompilerParams(vmem_limit_bytes=BIG),
+    )(place, spans, x.reshape(length, width), kv, qt, kt, qr, gctx, ctx32, pg, pg_in)
+
+
+def reduce_kernel(
+    src, gq, pr, dst, p_out, q_out,
+    gq_in, gq_sum, qa_in, qa_sum, qb_in, pa_in, pa_sum, pb_in, p_own, gq_own, pr_own,
+    lsem, send, recv, gsend, grecv, qasend, qarecv, qbsend, qbrecv, qcsend, qcrecv,
+    pasend, parecv, pbsend, pbrecv, pcsend, pcrecv,
+):
+    r, g, z, c = where_am_i()
+    greet(r, g, 4, 8)
+    pair = remote(gq.at[1 - c], gq_in, gsend, grecv, r, 2 * z + 1 - c)
+    pair.start()
+    waits = []
+    for d in range(1, 4):
+        rr = lax.rem(r + d, 4)
+        copy = remote(pr.at[rr], pa_in.at[r], pasend.at[d - 1], parecv.at[r], rr, g)
+        copy.start()
+        waits.append(copy)
+    own = pltpu.make_async_copy(src.at[g], dst.at[c, z], lsem.at[0])
+    own.start()
+    load_g = pltpu.make_async_copy(gq.at[c], gq_own, lsem.at[1])
+    load_g.start()
+    load_p = pltpu.make_async_copy(pr.at[r], pr_own, lsem.at[2])
+    load_p.start()
+    for d in range(1, 8):
+        to = lax.rem(g + d, 8)
+        copy = remote(src.at[to], dst.at[c, z], send.at[d - 1], recv.at[g], r, to)
+        copy.start()
+        waits.append(copy)
+
+    def f32(value):
+        return value.astype(jnp.float32)
+
+    load_g.wait()
+    pair.wait_recv()
+    gq_sum[...] = (f32(gq_own[...]) + f32(gq_in[...])).astype(jnp.bfloat16)
+    for d in range(1, 4):
+        rr = lax.rem(r + d, 4)
+        copy = remote(gq_sum.at[rr], qa_in.at[r], qasend.at[d - 1], qarecv.at[r], rr, g)
+        copy.start()
+        waits.append(copy)
+    load_p.wait()
+    for d in range(1, 4):
+        b = lax.rem(r + d, 4)
+        remote(pr.at[r], pa_in.at[b], pasend.at[0], parecv.at[b], b, g).wait_recv()
+    total = f32(pr_own[...])
+    for d in range(1, 4):
+        total = total + f32(pa_in[lax.rem(r + d, 4)])
+    pa_sum[...] = total.astype(jnp.bfloat16)
+    for d in range(1, 4):
+        zz = lax.rem(z + d, 4)
+        copy = remote(pa_sum.at[zz], pb_in.at[z], pbsend.at[d - 1], pbrecv.at[z], r, 2 * zz + c)
+        copy.start()
+        waits.append(copy)
+    for d in range(1, 4):
+        b = lax.rem(r + d, 4)
+        remote(gq_sum.at[r], qa_in.at[b], qasend.at[0], qarecv.at[b], b, g).wait_recv()
+    total = f32(gq_sum[r])
+    for d in range(1, 4):
+        total = total + f32(qa_in[lax.rem(r + d, 4)])
+    qa_sum[...] = total.astype(jnp.bfloat16)
+
+    @pl.when(z != r)
+    def _():
+        remote(qa_sum, qb_in.at[z], qbsend, qbrecv.at[z], r, 2 * r + c).start()
+
+    for d in range(1, 4):
+        b = lax.rem(z + d, 4)
+        remote(pa_sum.at[z], pb_in.at[b], pbsend.at[0], pbrecv.at[b], r, g).wait_recv()
+    total = f32(pa_sum[z])
+    for d in range(1, 4):
+        total = total + f32(pb_in[lax.rem(z + d, 4)])
+    p_own[...] = total.astype(jnp.bfloat16)
+    keep_p = pltpu.make_async_copy(p_own, p_out.at[r], lsem.at[3])
+    keep_p.start()
+    for d in range(1, 4):
+        rr = lax.rem(r + d, 4)
+        copy = remote(p_own, p_out.at[r], pcsend.at[d - 1], pcrecv.at[r], rr, g)
+        copy.start()
+        waits.append(copy)
+
+    @pl.when(z == r)
+    def _():
+        for d in range(1, 4):
+            b = lax.rem(z + d, 4)
+            remote(qa_sum, qb_in.at[b], qbsend, qbrecv.at[b], r, g).wait_recv()
+        qb_in[z] = qa_sum[...]
+        keep = pltpu.make_async_copy(qb_in, q_out, lsem.at[4])
+        keep.start()
+        for d in range(1, 4):
+            remote(qb_in, q_out, qcsend.at[d - 1], qcrecv, lax.rem(r + d, 4), g).start()
+        keep.wait()
+        for d in range(1, 4):
+            remote(qb_in, q_out, qcsend.at[d - 1], qcrecv, lax.rem(r + d, 4), g).wait_send()
+
+    @pl.when(z != r)
+    def _():
+        remote(qb_in, q_out, qcsend.at[0], qcrecv, r, g).wait_recv()
+        remote(qa_sum, qb_in.at[z], qbsend, qbrecv.at[z], r, 2 * r + c).wait_send()
+
+    for d in range(1, 4):
+        b = lax.rem(r + d, 4)
+        remote(p_own, p_out.at[b], pcsend.at[0], pcrecv.at[b], b, g).wait_recv()
+    for d in range(1, 8):
+        b = lax.rem(g + d, 8)
+        remote(src.at[g], dst.at[lax.rem(b, 2), lax.div(b, 2)], send.at[0], recv.at[b], r, b).wait_recv()
+    pair.wait_send()
+    for copy in waits:
+        copy.wait_send()
+    keep_p.wait()
+    own.wait()
+
+
+def reduce_all(src, gq, pr):
+    dma = pltpu.SemaphoreType.DMA
+    anywhere = pl.BlockSpec(memory_space=pl.ANY)
+    bf = jnp.bfloat16
+    width = gq.shape[-1]
+    return pl.pallas_call(
+        reduce_kernel,
+        name="reduce",
+        out_shape=(
+            jax.ShapeDtypeStruct((2, 4) + src.shape[1:], bf),
+            jax.ShapeDtypeStruct((4, 112, width), bf),
+            jax.ShapeDtypeStruct((4, 48, width), bf),
+        ),
+        in_specs=[anywhere] * 3,
+        out_specs=[anywhere] * 3,
+        scratch_shapes=[
+            pltpu.VMEM((4, 48, width), bf),
+            pltpu.VMEM((4, 48, width), bf),
+            pltpu.VMEM((4, 48, width), bf),
+            pltpu.VMEM((48, width), bf),
+            pltpu.VMEM((4, 48, width), bf),
+            pltpu.VMEM((4, 4, 112, width), bf),
+            pltpu.VMEM((4, 112, width), bf),
+            pltpu.VMEM((4, 112, width), bf),
+            pltpu.VMEM((112, width), bf),
+            pltpu.VMEM((4, 48, width), bf),
+            pltpu.VMEM((4, 112, width), bf),
+            dma((5,)), dma((7,)), dma((8,)), dma, dma, dma((3,)), dma((4,)), dma, dma((4,)),
+            dma((3,)), dma, dma((3,)), dma((4,)), dma((3,)), dma((4,)), dma((3,)), dma((4,)),
+        ],
+        compiler_params=pltpu.CompilerParams(
+            collective_id=4, has_side_effects=True, vmem_limit_bytes=BIG // 2
+        ),
+    )(src, gq, pr)
+
+
+def finish_kernel(
+    place, parts, grad_one, w, p_in, q_in,
+    out, g_q, g_k, g_v, g_o, g_in, g_up, rows_out, wq,
+):
+    seqs, rows, width = grad_one.shape
+    span = 96
+    for i in range(3):
+        for g in range(8):
+            wq[i, 48 * g : 48 * g + 48, :] = w[g % 2, g // 2, 48 * i : 48 * i + 48, :]
+    for s in range(seqs):
+        total = grad_one[s]
+        for i in range(3):
+            turned = jnp.concatenate(
+                [parts[s, z, i * span : (i + 1) * span, :] for z in range(4)], axis=0
+            )
+            back = turned.astype(jnp.float32).T.astype(jnp.bfloat16)
+            total = total + lax.dot_general(
+                back, wq[i], (((1,), (1,)), ((), ())), preferred_element_type=jnp.float32
+            )
+        out[s] = total.astype(jnp.bfloat16)
+    wide = [q_in[z].astype(jnp.float32) for z in range(4)]
+    for i, ref in enumerate((g_q, g_k, g_v)):
+        ref[...] = jnp.concatenate([v[:, i * span : (i + 1) * span] for v in wide], axis=1)
+    z = place[0]
+    mine = q_in[z].astype(jnp.float32)[:, 3 * span :]
+    rows_out[0:48, 0:96] = mine
+    rows_out[0:48, 96:384] = jnp.zeros((48, 288), jnp.float32)
+    rows_out[48:64, :] = p_in[3, 96:112, :].astype(jnp.float32)
+    g_o[...] = p_in[0, 0:48, :].astype(jnp.float32)
+    g_in[:, 0:384] = p_in[0, 48:96, :].astype(jnp.float32)
+    g_in[:, 384:768] = p_in[1, 0:48, :].astype(jnp.float32)
+    g_in[:, 768:1152] = p_in[1, 48:96, :].astype(jnp.float32)
+    g_in[:, 1152:1536] = p_in[2, 0:48, :].astype(jnp.float32)
+    g_up[0:16, :] = p_in[0, 96:112, :].astype(jnp.float32)
+    g_up[16:32, :] = p_in[1, 96:112, :].astype(jnp.float32)
+    g_up[32:96, :] = p_in[2, 48:112, :].astype(jnp.float32)
+    g_up[96:192, :] = p_in[3, 0:96, :].astype(jnp.float32)
+
+
+def finish(place, parts, grad_one, w, p_in, q_in):
+    seqs, rows, width = grad_one.shape
+    vm = pl.BlockSpec(memory_space=pltpu.VMEM)
+    sm = pl.BlockSpec(memory_space=pltpu.SMEM)
+    bf, f4 = jnp.bfloat16, jnp.float32
+    return pl.pallas_call(
+        finish_kernel,
+        name="finish",
+        out_shape=(
+            jax.ShapeDtypeStruct((seqs, rows, width), bf),
+            jax.ShapeDtypeStruct((48, width), f4),
+            jax.ShapeDtypeStruct((48, width), f4),
+            jax.ShapeDtypeStruct((48, width), f4),
+            jax.ShapeDtypeStruct((48, width), f4),
+            jax.ShapeDtypeStruct((48, 4 * width), f4),
+            jax.ShapeDtypeStruct((192, width), f4),
+            jax.ShapeDtypeStruct((64, width), f4),
+        ),
+        in_specs=[sm] + [vm] * 5,
+        out_specs=[vm] * 8,
+        scratch_shapes=[pltpu.VMEM((3, width, width), bf)],
+        compiler_params=pltpu.CompilerParams(vmem_limit_bytes=BIG),
+    )(place, parts, grad_one, w, p_in, q_in)
+
+
+def line_of_chips(
+    tokens, segment_ids, out_grad, query_weight, key_weight, value_weight, output_weight,
+    inner_weight, outer_weight, query_bias, value_bias, output_bias, inner_bias, outer_bias,
+    first_gain, first_shift, second_gain, second_shift,
+):
+    bf = jnp.bfloat16
+    width = tokens.shape[2]
+    g = lax.axis_index("grp")
+    z, c = lax.div(g, 2), lax.rem(g, 2)
+    place = jnp.stack([z, c]).astype(jnp.int32)
+    wp = jnp.concatenate(
+        [query_weight, key_weight, value_weight, output_weight]
+        + [inner_weight[:, j * width : (j + 1) * width] for j in range(4)]
+        + [outer_weight],
+        axis=0,
+    ).reshape(4, 144, width)
+    vectors = jnp.concatenate(
+        [query_bias, value_bias, output_bias, outer_bias, first_gain, first_shift, second_gain, second_shift]
+    )
+    small = jnp.concatenate(
+        [
+            jnp.pad(vectors, (0, 128))[None],
+            jnp.pad(inner_bias, (0, 320))[None],
+            segment_ids.astype(bf),
+            jnp.zeros((12, 512), bf),
+        ],
+        axis=0,
+    )
+    x, w, s = gather(tokens, wp, small)
+    vec = s[:, 0, :width].reshape(8, 8, 48).transpose(1, 0, 2).reshape(8, width)
+    inner_vec = s[:, 1, :192].reshape(1, 4 * width).astype(jnp.float32)
+    seg = jnp.where(c == 0, s[:, 2], s[:, 3]).astype(jnp.int32)
+    kv, qt, kt, qr, ctx, ctx32, spans = attend(place, x, w[0], vec, seg)
+    mine = exchange_context(ctx).reshape(2, width, -1)
+    layer_out, grad_one, gctx, pg = dense(
+        tokens, out_grad, mine, w, vec.astype(jnp.float32), inner_vec
+    )
+    gctx_in, pg_in = exchange_cotangent(gctx.reshape(2, 4, 96, -1), pg)
+    parts, gq, pr = attend_back(place, spans, x, kv, qt, kt, qr, gctx_in, ctx32, pg, pg_in)
+    parts_in, p_in, q_in = reduce_all(parts, gq, pr)
+    (input_grad, g_q, g_k, g_v, g_o, g_in, g_up, rows) = finish(
+        place, parts_in, grad_one, w[0], p_in, q_in
+    )
+    cols = lax.dynamic_slice_in_dim(rows[48:54], 48 * g, 48, 1)
+    inner_rows = rows[54:58].reshape(-1)
+    g_inner_bias = lax.dynamic_slice_in_dim(inner_rows, 192 * g, 192, 0)
+    return (
+        layer_out, input_grad, g_q, g_k, g_v, g_o, g_in, g_up,
+        rows[0:48, 0], rows[0:48, 1], cols[0], g_inner_bias, cols[1],
+        cols[2], cols[3], cols[4], cols[5],
+    )
+
+
 def solution(mesh):
     in_specs = (
         P("rep", "grp", None),
@@ -401,6 +1368,7 @@
         P("grp"),
         P("grp"),
     )
+    whole_line = mesh.shape["grp"] == 8 and mesh.shape["rep"] == 4
     return jax.shard_map(
-        on_device, mesh=mesh, in_specs=in_specs, out_specs=out_specs, check_vma=False
-    )
+        line_of_chips if whole_line else on_device, mesh=mesh, in_specs=in_specs, out_specs=out_specs, check_vma=False
+    )

time: 1730 us -> 455 us (0.26)
  matrix products: 697 us -> 0 us
  Pallas kernels: 0 us -> 420 us
  waiting for transfers between devices: 353 us -> 0 us
  other arithmetic: 321 us -> 2.26 us
  local copies, waits for them, and re-layouts: 174 us -> 27 us
  blocking collectives: 133 us -> 0 us
  loops' own time: 21.4 us -> 0 us
  between operations: 18.4 us -> 0.82 us
    dot_general x78 -> x0, matrix products: 697 us -> none  [the longest x12 165 us: masked_scores(): jnp.einsum('bqhd,bkhd->bhqk', query_group, key_group, preferred_element_t...]
    pallas_call x0 -> x8, Pallas kernels: none -> 420 us  [the longest x1 97.1 us: attend(): pl.pallas_call(attend_kernel, name='attend', out_shape=(jax.ShapeDtypeStr...]
    reduce_scatter x7 -> x0, waiting for transfers between devices: 203 us -> none  [the longest x2 128 us: on_device(): lax.psum_scatter(key_groups, 'grp', scatter_dimension=2, tiled=True)]
    convert_element_type x32 -> x4, other arithmetic: 192 us -> 1.5 us  [the longest x1 0.79 us: line_of_chips(): inner_vec = s[:, 1, :192].reshape(1, 4 * width).astype(jnp.float32)]
    reduce_sum x20 -> x0, other arithmetic: 106 us -> none  [the longest x6 90.9 us: group_forward(): jnp.sum(jnp.exp(scores - highest), axis=-1, keepdims=True)]
    psum x2 -> x0, waiting for transfers between devices: 93 us -> none  [the longest x1 49.5 us: on_device(): lax.psum(owned[0].astype(jnp.bfloat16), 'rep').astype(jnp.float32)]
    all_gather x5 -> x0, blocking collectives: 74.9 us -> none  [the longest x1 16.6 us: on_device(): lax.all_gather(output_weight, 'grp', axis=0, tiled=True)]
    unnamed x2 -> x0, blocking collectives: 58.4 us -> none
  transfers between devices with their start and end apart: 18 -> 0, of which waited for: 8 -> 0; matrix products, arithmetic and copies ran while one was open for 57% -> 0% of each run, Pallas kernels for 0% -> 0%
where the time goes in v1:
time: 455 us; the launch traced here: 450 us
  Pallas kernels  420 us (92%)
  local copies, waits for them, and re-layouts  27 us (6%)
    pallas_call x1, Pallas kernels, attend(): pl.pallas_call(attend_kernel, name='attend', out_shape=(jax.ShapeDtypeStr...  97.1 us
    pallas_call x1, Pallas kernels, reduce_all(): pl.pallas_call(reduce_kernel, name='reduce', out_shape=(jax.ShapeDtypeStr...  89.7 us
    pallas_call x1, Pallas kernels, attend_back(): pl.pallas_call(attend_back_kernel, name='attend_back', out_shape=(jax.Sha...  86.8 us
    pallas_call x1, Pallas kernels, gather(): pl.pallas_call(gather_kernel, name='gather', out_shape=(jax.ShapeDtypeStr...  67.4 us
    pallas_call x1, Pallas kernels, exchange_context(): pl.pallas_call(context_kernel, name='exchange_context', out_shape=jax.Sha...  29.3 us
    pallas_call x1, Pallas kernels, dense(): pl.pallas_call(dense_kernel, name='dense', out_shape=(jax.ShapeDtypeStruc...  24.7 us
    pallas_call x1, Pallas kernels, exchange_cotangent(): pl.pallas_call(cotangent_kernel, name='exchange_cotangent', out_shape=(ja...  20.3 us
    unnamed x30, local copies, waits for them, and re-layouts  14.5 us

profile of v1, /device:TPU:0, one launch (start us, length us, event | category | flops | bytes accessed | tf_op | source)
XLA Modules:
  0.0 449.7 jit_solution(13419853054474246055)
XLA Ops:
  0.7 0.1 pad_add_fusion.place
  0.7 0.8 constant_dynamic-update-slice_fusion.4
  1.5 0.8 constant_dynamic-update-slice_fusion.3
  2.3 0.8 constant_dynamic-update-slice_fusion.2
  3.1 0.8 constant_dynamic-update-slice_fusion.1
  3.8 0.8 slice_dynamic-update-slice_fusion.3
  4.6 0.8 slice_dynamic-update-slice_fusion.2
  5.4 0.8 slice_dynamic-update-slice_fusion.1
  6.2 0.8 slice_dynamic-update-slice_fusion
  7.0 0.9 constant_dynamic-update-slice_fusion
  7.9 0.0 copy-start.10
  7.9 5.5 %concatenate.10 = bf16[384]{0:T(512)(128)(2,1)S(1)} concatenate(bf16[48]{0:T(256)(128)(2,1)} %param.27, bf16[48]{0:T(256)(128)(2,1)} %param.28, bf16[48]{0:T(256)(128)(2,1)} %param.29, bf16[48]{0:T(256)(128)(2,1)} %param.31, bf16[48]{0:T(256)(128)(2,1)} %param.32, bf16[48]{0:T(256)(128)(2,1)} %param.33, bf16[48]{0:T(256)(128)(2,1)} %param.34, bf16[48]{0:T(256)(128)(2,1)} %param.35), dimensions={0} | concatenate | bytes 1536 | tf_op jit(solution)/shard_map/concatenate | solution.py:1294
  13.4 0.7 pad.9
  14.1 0.7 convert_element_type.20
  14.8 0.1 pad.13.clone
  14.8 0.7 maximum_maximum_fusion.small
  15.5 0.0 copy-done.10
  15.5 67.4 %gather.1 = (bf16[8,512,384]{2,1,0:T(8,128)(2,1)}, bf16[4,2,4,144,384]{4,3,2,1,0:T(8,128)(2,1)}, bf16[8,16,512]{2,1,0:T(8,128)(2,1)}) custom-call(bf16[2,512,384]{2,1,0:T(8,128)(2,1)} %tok.3, bf16[4,144,384]{2,1,0:T(8,128)(2,1)} %bitcast.30, bf16[16,512]{1,0:T(8,128)(2,1)} %maximum_maximum_fusion.small), custom_call_target="tpu_custom_call" | custom-call | tf_op jit(solution)/shard_map/gather/pallas_call | solution.py:522
  83.0 1.0 copy.39
  84.0 0.8 slice_reduce_fusion.2
  84.8 0.1 reshape_squeeze.4
  84.9 0.1 reshape.73.bias
  85.0 1.3 slice_bitcast_fusion.w
  86.3 0.0 copy-start
  86.3 0.0 copy-start.9
  86.3 97.1 %attend.1 = (bf16[3,4096,128]{2,1,0:T(8,128)(2,1)}, bf16[3,128,4096]{2,1,0:T(8,128)(2,1)}, bf16[3,32,4096]{2,1,0:T(8,128)(2,1)S(1)}, bf16[3,4096,128]{2,1,0:T(8,...) custom-call(s32[2]{0:T(128)S(1)} %pad_add_fusion.place, ...), custom_call_target="tpu_custom_call" | custom-call | tf_op jit(solution)/shard_map/attend/pallas_call | solution.py:694
  183.4 0.0 copy-start.4
  183.4 1.1 copy-done.4
  184.5 0.0 copy-start.8
  184.5 0.9 copy-done.8
  185.4 29.3 %exchange_context.1 = bf16[2,4,96,512]{3,2,1,0:T(8,128)(2,1)} custom-call(bf16[8,96,512]{2,1,0:T(8,128)(2,1)} %copy-done.8), custom_call_target="tpu_custom_call" | custom-call | tf_op jit(solution)/shard_map/exchange_context/pallas_call | solution.py:741
  214.7 0.8 convert_reduce_fusion
  215.5 0.1 reshape.78.inner_bias
  215.5 0.0 copy-done
  215.6 0.0 copy-done.9
  215.6 0.0 copy-start.1
  215.6 1.1 copy-done.1
  216.7 24.7 %dense.1 = (bf16[2,512,384]{2,1,0:T(8,128)(2,1)}, f32[2,512,384]{2,1,0:T(8,128)}, bf16[2,384,512]{2,1,0:T(8,128)(2,1)S(1)}, bf16[2,4,4,112,384]{4,3,2,1,0:T(8,128)(2,1)}) custom-call(bf16[2,512,384]{2,1,0:T(8,128)(2,1)S(1)} %copy-done, bf16[2,512,384]{2,1,0:T(8,128)(2,1)S(1)} %copy-done.9, bf16[2,384,512]{2,1,0:T(8,128)(2,1)S(1)} %bitcast.26, ...), custom_call_target="tpu_custom_call" | custom-call | tf_op jit(solution)/shard_map/dense/pallas_call | solution.py:913
  241.4 0.0 copy-start.7
  241.4 0.9 copy-done.7
  242.2 20.3 %exchange_cotangent.1 = (bf16[8,96,512]{2,1,0:T(8,128)(2,1)}, bf16[4,4,112,384]{3,2,1,0:T(8,128)(2,1)}) custom-call(bf16[2,4,96,512]{3,2,1,0:T(8,128)(2,1)} %bitcast.27, bf16[2,4,4,112,384]{4,3,2,1,0:T(8,128)(2,1)} %get-tuple-element.58.pg), custom_call_target="tpu_custom_call" | custom-call | tf_op jit(solution)/shard_map/exchange_cotangent/pallas_call | solution.py:779
  262.6 0.0 copy-start.6
  262.6 1.1 copy-done.6
  263.7 0.0 copy-start.5
  263.7 86.8 %attend_back.1 = (bf16[8,288,512]{2,1,0:T(8,128)(2,1)}, bf16[2,4,48,384]{3,2,1,0:T(8,128)(2,1)S(1)}, bf16[4,4,112,384]{3,2,1,0:T(8,128)(2,1)S(1)}) custom-call(s32[2]{0:T(128)S(1)} %pad_add_fusion.place, s32[2,16]{1,0:T(2,128)S(1)} %get-tuple-element.52.spans, bf16[4096,384]{1,0:T(8,128)(2,1)} %bitcast.29, bf16[3,4096,128]{2,1,0:T(8,128)(2,1)} %get-tuple-element.53.kv, ...), custom_call_target="tpu_custom_call" | custom-call | tf_op jit(solution)/shard_map/attend_back/pallas_call | solution.py:1047
  350.5 0.0 copy-start.2
  350.5 1.7 copy-done.2
  352.2 89.7 %reduce.9 = (bf16[2,4,288,512]{3,2,1,0:T(8,128)(2,1)S(1)}, bf16[4,112,384]{2,1,0:T(8,128)(2,1)S(1)}, bf16[4,48,384]{2,1,0:T(8,128)(2,1)S(1)}) custom-call(bf16[8,288,512]{2,1,0:T(8,128)(2,1)S(1)} %copy-done.2, bf16[2,4,48,384]{3,2,1,0:T(8,128)(2,1)S(1)} %get-tuple-element.63.gq, bf16[4,4,112,384]{3,2,1,0:T(8,128)(2,1)S(1)} %get-tuple-element.64.pr), custom_call_target="tpu_custom_call" | custom-call | tf_op jit(solution)/shard_map/reduce/pallas_call | solution.py:1183
  441.8 0.0 copy-start.3
  441.8 1.4 copy-done.3
  443.2 0.0 copy-done.5
  443.2 4.5 %finish.1 = (bf16[2,512,384]{2,1,0:T(8,128)(2,1)}, f32[48,384]{1,0:T(8,128)}, f32[48,384]{1,0:T(8,128)}, f32[48,384]{1,0:T(8,128)}, f32[48,384]{1,0:T(8,128)}, /...) custom-call(s32[2]{0:T(128)S(1)} %pad_add_fusion.place, bf16[2,4,288,512]{3,2,1,0:T(8,128)(2,1)} %copy-done.3, ...), custom_call_target="tpu_custom_call" | custom-call | tf_op jit(solution)/shard_map/finish/pallas_call | solution.py:1258
  447.8 0.6 dynamic_slice.7
  448.4 0.1 constant_dynamic-slice_fusion
  448.5 0.5 slice_bitcast_fusion.1
  449.0 0.7 slice_reduce_fusion
  (10 shorter events, 0.1 us)
Async XLA Ops:
  7.9 7.6 %copy-start.10 = (bf16[576,384]{1,0:T(8,128)(2,1)}, bf16[576,384]{1,0:T(8,128)(2,1)S(1)}, u32[]{:S(2)}) copy-start(bf16[576,384]{1,0:T(8,128)(2,1)S(1)} %constant_dynamic-update-slice_fusion) | copy-start | bytes 1327108
  86.3 129.3 %copy-start = (bf16[2,512,384]{2,1,0:T(8,128)(2,1)S(1)}, bf16[2,512,384]{2,1,0:T(8,128)(2,1)}, u32[]{:S(2)}) copy-start(bf16[2,512,384]{2,1,0:T(8,128)(2,1)} %tok.3) | copy-start | bytes 2359300
  86.3 129.3 %copy-start.9 = (bf16[2,512,384]{2,1,0:T(8,128)(2,1)S(1)}, bf16[2,512,384]{2,1,0:T(8,128)(2,1)}, u32[]{:S(2)}) copy-start(bf16[2,512,384]{2,1,0:T(8,128)(2,1)} %og.1) | copy-start | bytes 2359300
  183.4 1.1 copy-start.4
  184.5 0.9 copy-start.8
  215.6 1.1 copy-start.1
  241.4 0.9 copy-start.7
  262.6 1.1 copy-start.6
  263.7 179.5 %copy-start.5 = (f32[2,512,384]{2,1,0:T(8,128)S(1)}, f32[2,512,384]{2,1,0:T(8,128)}, u32[]{:S(2)}) copy-start(f32[2,512,384]{2,1,0:T(8,128)} %get-tuple-element.66.grad_one) | copy-start | bytes 4718596
  350.5 1.7 copy-start.2
  441.8 1.4 copy-start.3
